TPU v7x, 128 devices: a whole 4x4x4 slice. The times are simulated.
128 devices in a mesh: row: 8 (over z, core), col: 16 (over y, x).
Axes of the slice: x: 4, y: 4, z: 4, core: 2. Of those that a mesh axis runs over, the one named last changes fastest.
Arguments:
- tokens: bfloat16 [512, 8192], P('row', 'col'), may hold values from -6 to 6
- weights: bfloat16 [2, 8192, 28672], P(None, 'col', 'row'), may hold values from -2 to 2
- adapter_in: bfloat16 [2, 64, 8192], P(None, None, 'col'), may hold values from -0.75 to 0.75
- adapter_out: bfloat16 [2, 64, 28672], P(None, None, 'row'), may hold values from -0.3 to 0.3
- magnitude: float32 [2, 28672], P(None, 'row'), may hold values from 0.5 to 2
- hidden_cot: bfloat16 [512, 28672], P('col', 'row'), may hold values from -0.29882812 to 0.29882812
Outputs:
- hidden: bfloat16 [512, 28672], P('col', 'row')
- grad_in: float32 [2, 64, 8192], P(None, None, 'col')
- grad_out: float32 [2, 64, 28672], P(None, None, 'row')
- grad_mag: float32 [2, 28672], P(None, 'row')
All inputs are finite; a program needn't handle non-finite values.
Results may differ from a plain program's by a relative error of at most 0.028.
Values may be sent and summed in bfloat16 or wider, within the bound.
A program may use at most 192 MiB of HBM per device.

v0:
```python
import jax
import jax.numpy as jnp
from jax import lax
from jax.sharding import PartitionSpec as P

EPSILON = 1e-06


def copy_for_each(value, axis):
    copies = jnp.broadcast_to(value, (lax.axis_size(axis), *value.shape))
    return lax.all_to_all(copies, axis, split_axis=0, concat_axis=0, tiled=True)


def over_copies(value, axis):
    everything = copy_for_each(value, axis)
    return jnp.sum(everything, axis=0)


def laid_out(pieces, dim):
    lengths = list(pieces.shape[1:])
    lengths[dim] *= pieces.shape[0]
    return jnp.moveaxis(pieces, 0, dim).reshape(lengths)


def gathered_copies(value, axis, dim):
    return laid_out(copy_for_each(value, axis), dim)


def of_everyone(value, axis):
    return copy_for_each(value, axis).astype(jnp.float32).sum(axis=0)


def cotangents(gate, up_proj, cot_rows):
    sigmoid_g = jax.nn.sigmoid(gate)
    cot_float = cot_rows.astype(jnp.float32)
    d_gate = (cot_float * up_proj * sigmoid_g * (1.0 + gate * (1.0 - sigmoid_g))).astype(
        jnp.bfloat16
    )
    d_up = (cot_float * gate * sigmoid_g).astype(jnp.bfloat16)
    return (d_gate, d_up)


def on_device(tokens, weights, adapter_in, adapter_out, magnitude, hidden_cot):
    in_float = adapter_in.astype(jnp.float32)
    out_float = adapter_out.astype(jnp.float32)
    low_rank = jnp.einsum(
        "prd,prf->pdf", adapter_in, adapter_out, preferred_element_type=jnp.float32
    )
    direction = weights.astype(jnp.float32) + low_rank
    square_sum = over_copies(jnp.sum(direction * direction, axis=1), "col")
    column_norm = jnp.sqrt(square_sum + EPSILON)
    merged = (direction * (magnitude / column_norm)[:, None, :]).astype(jnp.bfloat16)
    token_all = gathered_copies(tokens, "row", 0)
    share_rows = token_all.shape[0] // lax.axis_size("col")
    partial_value = jnp.einsum("td,pdf->ptf", token_all, merged, preferred_element_type=jnp.float32)
    summed = lax.psum(partial_value.astype(jnp.bfloat16), "col").astype(jnp.float32)
    gate, up_proj = (summed[0], summed[1])
    hidden_all = (gate * jax.nn.sigmoid(gate) * up_proj).astype(jnp.bfloat16)
    hidden = lax.dynamic_slice_in_dim(hidden_all, lax.axis_index("col") * share_rows, share_rows, 0)
    cot_all = lax.all_gather(hidden_cot, "col", axis=0, tiled=True)
    d_gate, d_up = cotangents(gate, up_proj, cot_all)
    d_stack = jnp.stack((d_gate, d_up), axis=0)
    grad_weight = jnp.einsum("td,ptf->pdf", token_all, d_stack, preferred_element_type=jnp.float32)
    coef_grad = magnitude / column_norm
    statistic = over_copies(jnp.sum(grad_weight * direction, axis=1), "col")
    coef_dir = magnitude * statistic / column_norm**3
    d_direction = coef_grad[:, None, :] * grad_weight - coef_dir[:, None, :] * direction
    right_part = jnp.einsum("prd,pdf->prf", in_float, d_direction, precision=lax.Precision.HIGHEST)
    grad_out = lax.psum(right_part.astype(jnp.bfloat16), "col").astype(jnp.float32)
    left_part = jnp.einsum("prf,pdf->prd", out_float, d_direction, precision=lax.Precision.HIGHEST)
    grad_in = of_everyone(left_part.astype(jnp.bfloat16), "row").astype(jnp.float32)
    grad_mag = statistic / column_norm
    return (hidden, grad_in, grad_out, grad_mag)


def solution(mesh):
    in_specs = (
        P("row", "col"),
        P(None, "col", "row"),
        P(None, None, "col"),
        P(None, None, "row"),
        P(None, "row"),
        P("col", "row"),
    )
    out_specs = (P("col", "row"), P(None, None, "col"), P(None, None, "row"), P(None, "row"))
    return jax.shard_map(
        on_device, mesh=mesh, in_specs=in_specs, out_specs=out_specs, check_vma=False
    )
```

profile of v0, /device:TPU:1, one launch (start us, length us, event | category | flops | bytes accessed | tf_op | source)
XLA Modules:
  0.0 370.3 jit_solution(17381849521522753354)
XLA Ops:
  8.4 8.6 %multiply_reduce_fusion = (f32[2,3584]{1,0:T(2,128)S(1)}, f32[2,512,3584]{2,1,0:T(8,128)}) fusion(bf16[2,64,512]{2,1,0:T(8,128)(2,1)} %param.8, bf16[2,64,3584]{2,1,0:T(8,128)(2,1)S(1)} %copy-done, bf16[2,512,3584]{2,1,0:T(8,128)(2,1)} %param.7), kind=kOutput, calls=%fused_computation.5 | convolution fusion | flops 484434944 | bytes 23097344 | tf_op jit(solution)/shard_map/prd,prf->pdf/dot_general | solution.py:46
  17.1 19.1 %all_to_all.20 = f32[16,2,3584]{2,1,0:T(2,128)S(1)} all-to-all(f32[16,2,3584]{2,1,0:T(2,128)S(1)} %broadcast_in_dim.15), channel_id=1, replica_groups=mesh['row'=8,'col'=16] {'col'}, dimensions={0} | all-to-all | bytes 917504 | tf_op jit(solution)/shard_map/all_to_all | solution.py:11
  37.1 7.3 %all-to-all-start.1 = ((bf16[8,64,512]{2,1,0:T(8,128)(2,1)}), bf16[8,64,512]{2,1,0:T(8,128)(2,1)S(1)}, u32[]{:S(2)}, u32[]{:S(2)}) async-start(bf16[8,64,512]{2,1,0:T(8,128)(2,1)} %broadcast_in_dim.16), calls=%async_computation.1 | async-start | bytes 1048576 | tf_op jit(solution)/shard_map/all_to_all | solution.py:11
  44.6 9.1 %all-to-all-done.1 = bf16[8,64,512]{2,1,0:T(8,128)(2,1)S(1)} async-done(((bf16[8,64,512]{2,1,0:T(8,128)(2,1)}), bf16[8,64,512]{2,1,0:T(8,128)(2,1)S(1)}, u32[]{:S(2)}, u32[]{:S(2)}) %all-to-all-start.1) | async-done | bytes 524320 | tf_op jit(solution)/shard_map/all_to_all | solution.py:11
  53.7 11.6 %fusion.12 = bf16[2,512,3584]{1,2,0:T(8,128)(2,1)} fusion(bf16[512,512,1]{1,0,2:T(8,128)(2,1)S(1)} %bitcast.53, f32[2,512,3584]{2,1,0:T(8,128)} %get-tuple-element.28, f32[2,3584]{1,0:T(2,128)S(1)} %fusion.30), kind=kOutput, calls=%fused_computation.23 | convolution fusion | flops 3769106432 | bytes 22573056 | tf_op jit(solution)/shard_map/td,pdf->ptf/dot_general | solution.py:55
  65.9 5.9 %copy.27 = bf16[512,3584]{0,1:T(8,128)(2,1)} copy(bf16[512,3584]{1,0:T(8,128)(2,1)} %all-gather.2.cloned.1.call-done) | data formatting | bytes 7340032 | tf_op jit(solution)/shard_map/all_gather | solution.py:60
  71.8 128.4 %all-reduce.3.cloned.1.call-done = bf16[2,512,3584]{1,2,0:T(8,128)(2,1)} async-done(((bf16[2,512,3584]{1,2,0:T(8,128)(2,1)}), bf16[2,512,3584]{1,2,0:T(8,128)(2,1)}) %all-reduce.3.cloned.1.call-update) | async-done | bytes 7340048 | tf_op jit(solution)/shard_map/psum | solution.py:56
  200.2 10.3 %convert_element_type.51 = f32[2,512,3584]{1,2,0:T(8,128)} convert(bf16[2,512,3584]{1,2,0:T(8,128)(2,1)} %all-reduce.3.cloned.1.call-done) | non-fusion elementwise | flops 3670016 | bytes 22020096 | tf_op jit(solution)/shard_map/convert_element_type | solution.py:56
  210.5 9.8 %fusion.20 = (bf16[1,512,3584]{1,2,0:T(8,128)(2,1)S(1)}, bf16[1,512,3584]{1,2,0:T(8,128)(2,1)S(1)}, f32[512,3584]{0,1:T(8,128)}) fusion(bf16[512,3584]{0,1:T(8,128)(2,1)} %copy.27, f32[2,512,3584]{1,2,0:T(8,128)} %convert_element_type.51), kind=kLoop, calls=%fused_computation.28 | loop fusion | flops 25690112 | bytes 33030144 | tf_op jit(solution)/shard_map/stack | solution.py:62
  220.3 10.6 %fusion.1 = (f32[2,3584]{1,0:T(2,128)S(1)}, f32[2,3584,512]{1,2,0:T(8,128)}) fusion(f32[2,512,3584]{2,1,0:T(8,128)} %get-tuple-element.28, bf16[512,512,1]{1,0,2:T(8,128)(2,1)S(1)} %bitcast.54, bf16[1,512,3584]{1,2,0:T(8,128)(2,1)S(1)} %get-tuple-element.21, bf16[1,512,3584]{1,2,0:T(8,128)(2,1)S(1)} %get-tuple-element.20), kind=kOutput, calls=%fused_computation.3 | convolution fusion | flops 3769099264 | bytes 37253120 | tf_op jit(solution)/shard_map/td,ptf->pdf/dot_general | solution.py:63
  231.0 0.9 broadcast_in_dim.17
  231.9 5.1 %all-to-all-start.2 = ((f32[16,2,3584]{2,1,0:T(2,128)}), f32[16,2,3584]{2,1,0:T(2,128)S(1)}, u32[]{:S(2)}, u32[]{:S(2)}) async-start(f32[16,2,3584]{2,1,0:T(2,128)} %broadcast_in_dim.17), calls=%async_computation.2 | async-start | bytes 917504 | tf_op jit(solution)/shard_map/all_to_all | solution.py:11
  237.2 9.5 %all-to-all-done.2 = f32[16,2,3584]{2,1,0:T(2,128)S(1)} async-done(((f32[16,2,3584]{2,1,0:T(2,128)}), f32[16,2,3584]{2,1,0:T(2,128)S(1)}, u32[]{:S(2)}, u32[]{:S(2)}) %all-to-all-start.2) | async-done | bytes 458784 | tf_op jit(solution)/shard_map/all_to_all | solution.py:11
  247.5 1.4 fusion.29
  248.9 14.3 %fusion.25 = bf16[2,64,512]{2,1,0:T(8,128)(2,1)S(1)} fusion(bf16[2,64,3584]{2,1,0:T(8,128)(2,1)S(1)} %copy-done, f32[2,3584,512]{1,2,0:T(8,128)} %get-tuple-element.30, f32[2,512,3584]{2,1,0:T(8,128)} %get-tuple-element.28, f32[2,3584]{1,0:T(2,128)S(1)} %get-tuple-element.26, f32[2,3584]{1,0:T(2,128)S(1)} %fusion.30), kind=kOutput, calls=%fused_computation.34 | convolution fusion | flops 2829647872 | bytes 30466048 | tf_op jit(solution)/shard_map/prf,pdf->prd/dot_general | solution.py:70
  263.3 13.3 %fusion.16 = bf16[2,64,3584]{2,1,0:T(8,128)(2,1)} fusion(bf16[2,64,512]{2,1,0:T(8,128)(2,1)S(1)} %copy-done.1, f32[2,3584,512]{1,2,0:T(8,128)} %get-tuple-element.30, f32[2,512,3584]{2,1,0:T(8,128)S(1)} %bitcast.52, f32[2,3584]{1,0:T(2,128)S(1)} %get-tuple-element.26, f32[2,3584]{1,0:T(2,128)S(1)} %fusion.30), kind=kOutput, calls=%fused_computation.26 | convolution fusion | flops 2830041088 | bytes 30466048 | tf_op jit(solution)/shard_map/prd,pdf->prf/dot_general | solution.py:68
  276.6 1.2 broadcast_in_dim.18
  277.8 6.4 %all-to-all-start.3 = ((bf16[8,2,64,512]{3,2,1,0:T(8,128)(2,1)}), bf16[8,2,64,512]{3,2,1,0:T(8,128)(2,1)S(1)}, u32[]{:S(2)}, u32[]{:S(2)}) async-start(bf16[8,2,64,512]{3,2,1,0:T(8,128)(2,1)} %broadcast_in_dim.18), calls=%async_computation.3 | async-start | bytes 2097152 | tf_op jit(solution)/shard_map/all_to_all | solution.py:11
  284.2 12.4 %slice_bitcast_fusion.1 = (f32[512,3584]{0,1:T(8,128)}, f32[512,3584]{0,1:T(8,128)}) fusion(f32[2,512,3584]{1,2,0:T(8,128)} %convert_element_type.51), kind=kLoop, calls=%fused_computation.16 | loop fusion | bytes 29360128 | tf_op jit(solution)/shard_map/squeeze | solution.py:57
  296.6 4.1 %fusion.21 = bf16[32,3584]{0,1:T(8,128)(2,1)S(1)} fusion(f32[512,3584]{0,1:T(8,128)} %get-tuple-element.24, s32[]{:T(128)S(6)} %select_n.3, f32[512,3584]{0,1:T(8,128)} %get-tuple-element.22, f32[512,3584]{0,1:T(8,128)} %get-tuple-element.23), kind=kLoop, calls=%fused_computation.31 | loop fusion | flops 344064 | bytes 1605636 | tf_op jit(solution)/shard_map/convert_element_type | solution.py:58
  300.7 1.0 copy.31
  301.7 58.7 %all-reduce.5.cloned.1.call-done = bf16[2,64,3584]{2,1,0:T(8,128)(2,1)} async-done(((bf16[2,64,3584]{2,1,0:T(8,128)(2,1)}), bf16[2,64,3584]{2,1,0:T(8,128)(2,1)}) %all-reduce.5.cloned.1.call-update) | async-done | bytes 917520 | tf_op jit(solution)/shard_map/psum | solution.py:69
  360.3 2.6 convert_element_type.61
  362.9 0.8 convert_reduce_fusion
  (30 shorter events, 3.9 us)
Async XLA Ops:
  7.2 1.2 copy-start
  7.2 58.7 %all-gather.2.cloned.1.call-start = ((), (), s32[]{:S(2)}) async-start(), calls=%async_computation.5 | async-start | bytes 3899392 | tf_op jit(solution)/shard_map/all_gather | solution.py:60
  8.4 27.9 %copy-start.3 = (bf16[64,512]{1,0:T(8,128)(2,1)S(1)}, bf16[64,512]{1,0:T(8,128)(2,1)}, u32[]{:S(2)}) copy-start(bf16[64,512]{1,0:T(8,128)(2,1)} %param.6) | copy-start | bytes 196612
  8.4 36.2 %copy-start.2 = (f32[2,3584]{1,0:T(2,128)S(1)}, f32[2,3584]{1,0:T(2,128)}, u32[]{:S(2)}) copy-start(f32[2,3584]{1,0:T(2,128)} %param.10) | copy-start | bytes 86020
  37.1 16.7 %all-to-all-start.1 = ((bf16[8,64,512]{2,1,0:T(8,128)(2,1)}), bf16[8,64,512]{2,1,0:T(8,128)(2,1)S(1)}, u32[]{:S(2)}, u32[]{:S(2)}) async-start(bf16[8,64,512]{2,1,0:T(8,128)(2,1)} %broadcast_in_dim.16), calls=%async_computation.1 | async-start | bytes 1048576 | tf_op jit(solution)/shard_map/all_to_all | solution.py:11
  44.4 155.8 %all-reduce.3.cloned.1.call-start = ((), (), s32[]{:S(2)}) async-start(), calls=%async_computation.4 | async-start | bytes 14680064 | tf_op jit(solution)/shard_map/psum | solution.py:56
  231.0 32.3 %slice-start = ((s8[14680064]{0:T(1024)(128)(4,1)}), s8[2097152]{0:T(1024)(128)(4,1)S(1)}, s32[]{:S(2)}) async-start(s8[14680064]{0:T(1024)(128)(4,1)} %bitcast.51), calls=%async_computation.7 | async-start | bytes 4194304
  231.9 14.9 %all-to-all-start.2 = ((f32[16,2,3584]{2,1,0:T(2,128)}), f32[16,2,3584]{2,1,0:T(2,128)S(1)}, u32[]{:S(2)}, u32[]{:S(2)}) async-start(f32[16,2,3584]{2,1,0:T(2,128)} %broadcast_in_dim.17), calls=%async_computation.2 | async-start | bytes 917504 | tf_op jit(solution)/shard_map/all_to_all | solution.py:11
  237.0 123.4 %all-reduce.5.cloned.1.call-start = ((), (), s32[]{:S(2)}) async-start(), calls=%async_computation.6 | async-start | bytes 1835008 | tf_op jit(solution)/shard_map/psum | solution.py:69
  248.9 14.4 %slice-start.1 = ((s8[14680064]{0:T(1024)(128)(4,1)}), s8[4194304]{0:T(1024)(128)(4,1)S(1)}, s32[]{:S(2)}) async-start(s8[14680064]{0:T(1024)(128)(4,1)} %bitcast.51), calls=%async_computation.8 | async-start | bytes 8388608
  248.9 14.4 %slice-start.2 = ((s8[14680064]{0:T(1024)(128)(4,1)}), s8[4194304]{0:T(1024)(128)(4,1)S(1)}, s32[]{:S(2)}) async-start(s8[14680064]{0:T(1024)(128)(4,1)} %bitcast.51), calls=%async_computation.9 | async-start | bytes 8388608
  248.9 14.4 %slice-start.3 = ((s8[14680064]{0:T(1024)(128)(4,1)}), s8[4194304]{0:T(1024)(128)(4,1)S(1)}, s32[]{:S(2)}) async-start(s8[14680064]{0:T(1024)(128)(4,1)} %bitcast.51), calls=%async_computation.10 | async-start | bytes 8388608
  248.9 14.4 %copy-start.1 = (bf16[2,64,512]{2,1,0:T(8,128)(2,1)S(1)}, bf16[2,64,512]{2,1,0:T(8,128)(2,1)}, u32[]{:S(2)}) copy-start(bf16[2,64,512]{2,1,0:T(8,128)(2,1)} %param.8) | copy-start | bytes 393220
  277.8 85.1 %all-to-all-start.3 = ((bf16[8,2,64,512]{3,2,1,0:T(8,128)(2,1)}), bf16[8,2,64,512]{3,2,1,0:T(8,128)(2,1)S(1)}, u32[]{:S(2)}, u32[]{:S(2)}) async-start(bf16[8,2,64,512]{3,2,1,0:T(8,128)(2,1)} %broadcast_in_dim.18), calls=%async_computation.3 | async-start | bytes 2097152 | tf_op jit(solution)/shard_map/all_to_all | solution.py:11
Sparse Core Ops, SparseCore 0:
  10.1 55.6 all-gather.1
  69.3 130.8 all-reduce.2
  276.8 83.5 all-reduce.4
where the time goes:
time: 372 us; the launch traced here: 370 us
  waiting for transfers between devices  207 us (56%)
  matrix products  58.4 us (16%)
  other arithmetic  30.1 us (8%)
  local copies, waits for them, and re-layouts  22.7 us (6%)
  starting transfers between devices  19.1 us (5%)
  blocking collectives  19.1 us (5%)
  between operations  13.9 us (4%)
    psum x1, waiting for transfers between devices, on_device(): lax.psum(partial_value.astype(jnp.bfloat16), 'col').astype(jnp.float32)  128 us
    psum x1, waiting for transfers between devices, on_device(): lax.psum(right_part.astype(jnp.bfloat16), 'col').astype(jnp.float32)  58.7 us
    all_to_all x1, blocking collectives, copy_for_each(): return lax.all_to_all(copies, axis, split_axis=0, concat_axis=0, tiled=True)  19.1 us
    all_to_all x3, starting transfers between devices, copy_for_each(): return lax.all_to_all(copies, axis, split_axis=0, concat_axis=0, tiled=True)  18.8 us
    all_to_all x3, waiting for transfers between devices, copy_for_each(): return lax.all_to_all(copies, axis, split_axis=0, concat_axis=0, tiled=True)  18.7 us
    dot_general x1, matrix products, on_device(): jnp.einsum('prf,pdf->prd', out_float, d_direction, precision=lax.Precisio...  14.3 us
    dot_general x1, matrix products, on_device(): jnp.einsum('prd,pdf->prf', in_float, d_direction, precision=lax.Precision...  13.3 us
    squeeze x1, local copies, waits for them, and re-layouts, on_device(): gate, up_proj = (summed[0], summed[1])  12.4 us
  transfers between devices with their start and end apart: 6, of which 5 were waited for; matrix products, arithmetic and copies ran while one was open for 13% of the time, Pallas kernels for 0%

commit v1 on v0

v1 whole, which is shorter than its diff:
```python
import jax
import jax.numpy as jnp
from jax import lax
from jax.sharding import PartitionSpec as P

EPSILON = 1e-06
F32 = jnp.float32
BF16 = jnp.bfloat16


def on_device(tokens, weights, adapter_in, adapter_out, magnitude, hidden_cot):
    token_all = lax.all_gather(tokens, "row", axis=0, tiled=True)
    low_rank = jnp.einsum("prd,prf->pdf", adapter_in, adapter_out, preferred_element_type=F32)
    direction = weights.astype(F32) + low_rank
    square_sum = lax.psum(jnp.sum(direction * direction, axis=1), "col")
    direction_b = direction.astype(BF16)
    partial_value = jnp.einsum("td,pdf->ptf", token_all, direction_b, preferred_element_type=F32)
    raw = lax.psum_scatter(
        partial_value.astype(BF16), "col", scatter_dimension=1, tiled=True
    ).astype(F32)
    rank_tok = jnp.einsum("prd,td->prt", adapter_in, token_all, preferred_element_type=F32)
    rank_own = lax.psum_scatter(rank_tok, "col", scatter_dimension=2, tiled=True)
    column_norm = jnp.sqrt(square_sum + EPSILON)
    coef = magnitude / column_norm
    gate = raw[0] * coef[0]
    up = raw[1] * coef[1]
    sig = jax.nn.sigmoid(gate)
    hidden = (gate * sig * up).astype(BF16)
    cot = hidden_cot.astype(F32)
    d_gate = (cot * up * sig * (1.0 + gate * (1.0 - sig))).astype(BF16)
    d_up = (cot * gate * sig).astype(BF16)
    d_pre = jnp.stack((d_gate, d_up), axis=0)
    statistic = lax.psum(jnp.sum(d_pre.astype(F32) * raw, axis=1), "col")
    grad_mag = statistic / column_norm
    coef_dir = magnitude * statistic / column_norm**3
    first = jnp.einsum("prt,ptf->prf", rank_own.astype(BF16), d_pre, preferred_element_type=F32)
    second = jnp.einsum("prd,pdf->prf", adapter_in, direction_b, preferred_element_type=F32)
    grad_out = lax.psum(
        (coef[:, None, :] * first - coef_dir[:, None, :] * second).astype(BF16), "col"
    ).astype(F32)
    out_f = adapter_out.astype(F32)
    scaled = (out_f * coef[:, None, :]).astype(BF16)
    row_tok = jnp.einsum("prf,ptf->prt", scaled, d_pre, preferred_element_type=F32)
    row_all = lax.all_gather(row_tok.astype(BF16), "col", axis=2, tiled=True)
    left = jnp.einsum("prt,td->prd", row_all, token_all, preferred_element_type=F32)
    tilted = (out_f * coef_dir[:, None, :]).astype(BF16)
    left = left - jnp.einsum("prf,pdf->prd", tilted, direction_b, preferred_element_type=F32)
    grad_in = lax.psum(left.astype(BF16), "row").astype(F32)
    return (hidden, grad_in, grad_out, grad_mag)


def solution(mesh):
    in_specs = (
        P("row", "col"),
        P(None, "col", "row"),
        P(None, None, "col"),
        P(None, None, "row"),
        P(None, "row"),
        P("col", "row"),
    )
    out_specs = (P("col", "row"), P(None, None, "col"), P(None, None, "row"), P(None, "row"))
    return jax.shard_map(
        on_device, mesh=mesh, in_specs=in_specs, out_specs=out_specs, check_vma=False
    )
```

time: 372 us -> 456 us (1.23)
  blocking collectives: 19.1 us -> 152 us
  matrix products: 58.4 us -> 26.5 us
  other arithmetic: 30.1 us -> 7.55 us
  waiting for transfers between devices: 207 us -> 229 us
  starting transfers between devices: 19.1 us -> 0.16 us
    psum x0 -> x2, blocking collectives: none -> 121 us  [the longest x1 62.4 us: on_device(): square_sum = lax.psum(jnp.sum(direction * direction, axis=1), 'col')]
    unnamed x3 -> x5, waiting for transfers between devices: 0.71 us -> 67.8 us
    all_gather x0 -> x2, blocking collectives: none -> 31.6 us  [the longest x1 15.9 us: on_device(): token_all = lax.all_gather(tokens, 'row', axis=0, tiled=True)]
    dot_general x4 -> x7, matrix products: 49.8 us -> 21.2 us  [the longest x1 6.2 us: on_device(): jnp.einsum('td,pdf->ptf', token_all, direction_b, preferred_element_type=...]
    psum x2, waiting for transfers between devices: 187 us -> 161 us  [the longest x1 87.2 us: on_device(): lax.psum((coef[:, None, :] * first - coef_dir[:, None, :] * second).astyp...]
    all_to_all x1 -> x0, blocking collectives: 19.1 us -> none  [copy_for_each(): return lax.all_to_all(copies, axis, split_axis=0, concat_axis=0, tiled=True)]
    convert_element_type x0 -> x1, local copies, waits for them, and re-layouts: none -> 19 us  [on_device(): partial_value.astype(BF16)]
    all_to_all x3 -> x0, starting transfers between devices: 18.8 us -> none  [copy_for_each(): return lax.all_to_all(copies, axis, split_axis=0, concat_axis=0, tiled=True)]
  transfers between devices with their start and end apart: 6 -> 4, of which waited for: 5 -> 3; matrix products, arithmetic and copies ran while one was open for 13% -> 5% of each run, Pallas kernels for 0% -> 0%
where the time goes in v1:
time: 456 us; the launch traced here: 454 us
  waiting for transfers between devices  229 us (50%)
  blocking collectives  152 us (33%)
  matrix products  26.5 us (6%)
  local copies, waits for them, and re-layouts  24 us (5%)
  between operations  14.6 us (3%)
  other arithmetic  7.55 us (2%)
    psum x1, waiting for transfers between devices, on_device(): lax.psum((coef[:, None, :] * first - coef_dir[:, None, :] * second).astyp...  87.2 us
    psum x1, waiting for transfers between devices, on_device(): grad_in = lax.psum(left.astype(BF16), 'row').astype(F32)  74.2 us
    unnamed x5, waiting for transfers between devices  67.8 us
    psum x1, blocking collectives, on_device(): square_sum = lax.psum(jnp.sum(direction * direction, axis=1), 'col')  62.4 us
    psum x1, blocking collectives, on_device(): statistic = lax.psum(jnp.sum(d_pre.astype(F32) * raw, axis=1), 'col')  58.2 us
    convert_element_type x1, local copies, waits for them, and re-layouts, on_device(): partial_value.astype(BF16)  19 us
    all_gather x1, blocking collectives, on_device(): token_all = lax.all_gather(tokens, 'row', axis=0, tiled=True)  15.9 us
    all_gather x1, blocking collectives, on_device(): row_all = lax.all_gather(row_tok.astype(BF16), 'col', axis=2, tiled=True)  15.8 us
  transfers between devices with their start and end apart: 4, of which 3 were waited for; matrix products, arithmetic and copies ran while one was open for 5% of the time, Pallas kernels for 0%

profile of v1, /device:TPU:1, one launch (start us, length us, event | category | flops | bytes accessed | tf_op | source)
XLA Modules:
  0.0 454.1 jit_solution(2364083488424929774)
XLA Ops:
  7.2 15.9 %all_gather.6 = bf16[512,512]{1,0:T(8,128)(2,1)S(1)} all-gather(bf16[64,512]{1,0:T(8,128)(2,1)} %param.6), channel_id=1, replica_groups=mesh['row'=8,'col'=16] {'row'}, dimensions={0}, use_global_device_ids=true | all-gather | bytes 589824 | tf_op jit(solution)/shard_map/all_gather | solution.py:12
  23.1 5.3 %multiply_reduce_fusion = (f32[2,3584]{1,0:T(2,128)S(1)}, bf16[2,512,3584]{2,1,0:T(8,128)(2,1)S(1)}) fusion(bf16[2,512,3584]{2,1,0:T(8,128)(2,1)} %param.7, bf16[2,64,512]{2,1,0:T(8,128)(2,1)S(1)} %copy-done, bf16[2,64,3584]{2,1,0:T(8,128)(2,1)} %param.9), kind=kOutput, calls=%fused_computation | convolution fusion | flops 488104960 | bytes 15757312 | tf_op jit(solution)/shard_map/prd,prf->pdf/dot_general | solution.py:13
  28.4 3.0 copy-done.1
  31.4 6.2 %fusion.1 = bf16[2,512,3584]{1,2,0:T(8,128)(2,1)} fusion(bf16[2,512,3584]{2,1,0:T(8,128)(2,1)S(1)} %get-tuple-element.11, bf16[512,512]{1,0:T(8,128)(2,1)S(1)} %all_gather.6), kind=kOutput, calls=%fused_computation.4 | convolution fusion | flops 3761766400 | bytes 15204352 | tf_op jit(solution)/shard_map/td,pdf->ptf/dot_general | solution.py:17
  37.6 19.0 %copy.19 = bf16[2,512,3584]{2,0,1:T(2,128)(2,1)} copy(bf16[2,512,3584]{1,2,0:T(8,128)(2,1)} %fusion.1) | data formatting | bytes 14680064 | tf_op jit(solution)/shard_map/convert_element_type | solution.py:19
  56.6 1.1 fusion.12
  57.8 62.4 %psum.28 = f32[2,3584]{1,0:T(2,128)S(1)} all-reduce(f32[2,3584]{1,0:T(2,128)S(1)} %get-tuple-element.10), channel_id=1, replica_groups=mesh['row'=8,'col'=16] {'col'}, use_global_device_ids=true, to_apply=%region_2.0 | all-reduce | flops 7168 | bytes 57344 | tf_op jit(solution)/shard_map/psum | solution.py:15
  120.4 0.6 dynamic-slice
  121.6 67.7 %all-reduce.9.cloned.1.call-done = bf16[2,512,3584]{2,0,1:T(2,128)(2,1)} async-done(((bf16[2,512,3584]{2,0,1:T(2,128)(2,1)}), bf16[2,512,3584]{2,0,1:T(2,128)(2,1)}) %all-reduce.9.cloned.1.call-update) | async-done | bytes 7340048
  189.4 1.3 constant_dynamic-slice_fusion
  190.8 1.0 fusion.25
  191.8 0.8 multiply_reduce_fusion.1
  192.6 1.7 convolution_convert_fusion.1
  194.2 58.2 %psum.29 = f32[2,3584]{1,0:T(2,128)} all-reduce(f32[2,3584]{1,0:T(2,128)} %multiply_reduce_fusion.1), channel_id=1, replica_groups=mesh['row'=8,'col'=16] {'col'}, use_global_device_ids=true, to_apply=%region_4.0 | all-reduce | flops 7168 | bytes 57344 | tf_op jit(solution)/shard_map/psum | solution.py:33
  252.5 1.5 fusion.28
  253.9 5.9 %fusion.3 = f32[2,64,3584]{2,1,0:T(8,128)} fusion(bf16[2,64,512]{2,1,0:T(8,128)(2,1)S(1)} %copy-done, bf16[2,512,3584]{2,1,0:T(8,128)(2,1)} %copy-done.1, f32[2,3584]{1,0:T(2,128)S(1)} %get-tuple-element.16), kind=kOutput, calls=%fused_computation.8 | convolution fusion | flops 470220800 | bytes 9334784 | tf_op jit(solution)/shard_map/prd,pdf->prf/dot_general | solution.py:37
  259.8 15.8 %all_gather.7 = bf16[2,64,512]{1,2,0:T(8,128)(2,1)S(1)} all-gather(bf16[2,64,32]{1,2,0:T(8,128)(2,1)S(1)} %convolution_convert_fusion.1), channel_id=1, replica_groups=mesh['row'=8,'col'=16] {'col'}, dimensions={2}, use_global_device_ids=true | all-gather | bytes 139264 | tf_op jit(solution)/shard_map/all_gather | solution.py:44
  275.6 0.3 fusion.14
  275.9 3.0 fusion.7
  279.0 3.0 fusion.4
  282.0 74.2 %all-reduce.5.cloned.1.call-done = bf16[2,64,512]{2,1,0:T(8,128)(2,1)} async-done(((bf16[2,64,512]{2,1,0:T(8,128)(2,1)}), bf16[2,64,512]{2,1,0:T(8,128)(2,1)}) %all-reduce.5.cloned.1.call-update) | async-done | bytes 131088 | tf_op jit(solution)/shard_map/psum | solution.py:48
  356.2 1.6 convert_element_type.72
  357.9 87.2 %all-reduce.7.cloned.1.call-done = bf16[2,64,3584]{2,1,0:T(8,128)(2,1)} async-done(((bf16[2,64,3584]{2,1,0:T(8,128)(2,1)}), bf16[2,64,3584]{2,1,0:T(8,128)(2,1)}) %all-reduce.7.cloned.1.call-update) | async-done | bytes 917520 | tf_op jit(solution)/shard_map/psum | solution.py:38
  445.0 2.6 convert_element_type.75
  (36 shorter events, 0.5 us)
Async XLA Ops:
  7.2 15.9 %copy-start = (bf16[2,64,512]{2,1,0:T(8,128)(2,1)S(1)}, bf16[2,64,512]{2,1,0:T(8,128)(2,1)}, u32[]{:S(2)}) copy-start(bf16[2,64,512]{2,1,0:T(8,128)(2,1)} %param.8) | copy-start | bytes 393220
  7.2 182.2 %all-reduce.9.cloned.1.call-start = ((), (), s32[]{:S(2)}) async-start(), calls=%async_computation.4 | async-start | bytes 14680064
  23.1 33.5 %copy-start.2 = (bf16[512,512]{1,0:T(8,128)(2,1)}, bf16[512,512]{1,0:T(8,128)(2,1)S(1)}, u32[]{:S(2)}) copy-start(bf16[512,512]{1,0:T(8,128)(2,1)S(1)} %all_gather.6) | copy-start | bytes 1572868
  28.4 3.0 copy-start.1
  56.5 63.7 %copy-start.8 = (f32[2,3584]{1,0:T(2,128)S(1)}, f32[2,3584]{1,0:T(2,128)}, u32[]{:S(2)}) copy-start(f32[2,3584]{1,0:T(2,128)} %param.10) | copy-start | bytes 86020
  56.5 63.9 %copy-start.9 = (u32[128]{0:T(128)S(1)}, u32[128]{0:T(128)}, u32[]{:S(2)}) copy-start(u32[128]{0:T(128)} %constant.8) | copy-start | bytes 1540
  56.5 134.2 %copy-start.7 = (bf16[32,3584]{1,0:T(8,128)(2,1)S(1)}, bf16[32,3584]{1,0:T(8,128)(2,1)}, u32[]{:S(2)}) copy-start(bf16[32,3584]{1,0:T(8,128)(2,1)} %param.11) | copy-start | bytes 688132
  56.6 222.4 %reduce-scatter.2.cloned.1.call-start = ((), (), s32[]{:S(2)}) async-start(), calls=%async_computation.2 | async-start | bytes 557056 | tf_op jit(solution)/shard_map/reduce_scatter | solution.py:22
  57.8 298.4 %all-reduce.5.cloned.1.call-start = ((), (), s32[]{:S(2)}) async-start(), calls=%async_computation.1 | async-start | bytes 262144 | tf_op jit(solution)/shard_map/psum | solution.py:48
  120.3 71.5 %copy-start.6 = (f32[2,3584]{1,0:T(2,128)}, f32[2,3584]{1,0:T(2,128)S(1)}, u32[]{:S(2)}) copy-start(f32[2,3584]{1,0:T(2,128)S(1)} %psum.28) | copy-start | bytes 86020
  191.8 0.8 copy-start.4
  192.5 83.3 %slice-start = ((s8[7340032]{0:T(1024)(128)(4,1)}), s8[3145728]{0:T(1024)(128)(4,1)S(1)}, s32[]{:S(2)}) async-start(s8[7340032]{0:T(1024)(128)(4,1)} %bitcast.48), calls=%async_computation.5 | async-start | bytes 6291456
  253.9 21.6 %copy-start.3 = (bf16[512,512]{1,0:T(8,128)(2,1)S(1)}, bf16[512,512]{1,0:T(8,128)(2,1)}, u32[]{:S(2)}) copy-start(bf16[512,512]{1,0:T(8,128)(2,1)} %copy-done.2) | copy-start | bytes 1572868
  253.9 21.9 %slice-start.1 = ((s8[7340032]{0:T(1024)(128)(4,1)}), s8[4194304]{0:T(1024)(128)(4,1)S(1)}, s32[]{:S(2)}) async-start(s8[7340032]{0:T(1024)(128)(4,1)} %bitcast.48), calls=%async_computation.6 | async-start | bytes 8388608
  253.9 21.9 %copy-start.5 = (bf16[2,64,3584]{2,1,0:T(8,128)(2,1)S(1)}, bf16[2,64,3584]{2,1,0:T(8,128)(2,1)}, u32[]{:S(2)}) copy-start(bf16[2,64,3584]{2,1,0:T(8,128)(2,1)} %param.9) | copy-start | bytes 2752516
  278.9 166.1 %all-reduce.7.cloned.1.call-start = ((), (), s32[]{:S(2)}) async-start(), calls=%async_computation.3 | async-start | bytes 1835008 | tf_op jit(solution)/shard_map/psum | solution.py:38
Sparse Core Ops, SparseCore 0:
  56.7 132.6 all-reduce.8
  192.5 71.6 reduce-scatter.1
  279.0 77.1 all-reduce.4
  359.4 85.5 all-reduce.6

commit v2 on v1

v2 whole, which is shorter than its diff:
```python
import functools

import jax
import jax.numpy as jnp
from jax import lax
from jax.experimental import pallas as pl
from jax.experimental.pallas import tpu as pltpu
from jax.sharding import PartitionSpec as P

EPSILON = 1e-06
F32 = jnp.float32
BF16 = jnp.bfloat16
MESH = pl.DeviceIdType.MESH
SIDE = 4
ORDER = (2, 1, 3, 0)
EXCHANGES = 17
FAR, RAW, ACC = 0, 1, 2


def nt_dot(a, b):
    return lax.dot_general(a, b, (((1,), (1,)), ((), ())), preferred_element_type=F32)


def kernel(n_row, tok, w_hbm, ain, aout, mag, cot, hid, gi, go, gm,
           lhs, wb, pp, ain_t, rfar, rnear, sfar, snear, cotq, ssb, ssx, ssr, ssr2,
           zb, zx, zs, zr, zr2, hidq, hidr, dsc, st, strr, bb, ball, g1, g1r,
           wv, wx, wr, wall, gall0, gall1, gib, gir, gio, giall,
           w_sem, tok_s, tok_r, main_s, main_r, ph2_s, ph2_r, ex_s, ex_r):
    row, col = lax.axis_index("row"), lax.axis_index("col")
    y, x = col // SIDE, col % SIDE
    n_z = n_row // 2
    z, core = row // 2, row % 2
    share, depth = tok.shape
    rank = ain.shape[1]
    width = aout.shape[2]
    fq = width // SIDE
    tb = share * n_row // SIDE
    rq = rank // SIDE
    rb = tb + rq
    own_rows = tb // SIDE
    half = ((rb // 16 + 1) // 2) * 16
    top, bottom = pl.ds(0, half), pl.ds(half, rb - half)
    first, second = (x, y), (y, x)

    def wrap(v):
        return (v + 2 * SIDE) % SIDE

    def at_x(k):
        return (row, y * SIDE + wrap(x + k))

    def at_y(k):
        return (row, wrap(y + k) * SIDE + x)

    def at_row(k):
        return ((row + k) % n_row, col)

    def at_core():
        return (z * 2 + (1 - core), col)

    def at_z(k):
        return (((z + k) % n_z) * 2 + core, col)

    ring1 = (at_x, at_y)
    ring2 = (at_y, at_x)

    def w_copy(p, q):
        lanes = pl.ds(pl.multiple_of(q * fq, 128), fq)
        return pltpu.make_async_copy(w_hbm.at[p, :, lanes], wb.at[p, q], w_sem.at[p * SIDE + q])

    for j in ORDER:
        for p in range(2):
            w_copy(p, wrap(x + j)).start()

    barrier = pltpu.get_barrier_semaphore()
    peers = [at_x(k) for k in (1, 2, 3)] + [at_y(k) for k in (1, 2, 3)]
    peers += [at_row(k) for k in range(1, n_row)]
    for peer in peers:
        pl.semaphore_signal(barrier, inc=1, device_id=peer, device_id_type=MESH)
    pl.semaphore_wait(barrier, len(peers))

    def remote(src, dst, send, recv, peer):
        return pltpu.make_async_remote_copy(
            src_ref=src, dst_ref=dst, send_sem=send, recv_sem=recv,
            device_id=peer, device_id_type=MESH)

    def tok_rows(owner):
        start = owner * share
        offset = (start // tb) * rb + start % tb
        return lhs.at[0, pl.ds(pl.multiple_of(offset, 16), share), :]

    def tok_copy(i):
        if i == 0:
            src, dst, peer = tok, tok_rows(row), at_core()
        elif i < n_z:
            src, dst, peer = tok, tok_rows(row), at_z(i)
        else:
            owner = ((z + n_z - (i - n_z + 1)) % n_z) * 2 + core
            src, dst, peer = tok_rows(owner), tok_rows(owner), at_core()
        return remote(src, dst, tok_s.at[i], tok_r.at[i], peer)

    n_tok = 2 * n_z - 1
    for i in [1, n_z - 1] + list(range(2, n_z - 1)) + [0]:
        tok_copy(i).start()

    def exchange(e, peer_of, count, src, dst):
        return [remote(src(k), dst(k), ex_s.at[e * 8 + k], ex_r.at[e * 8 + k], peer_of(k))
                for k in range(1, count)]

    started = []

    def begin(copies):
        for c in copies:
            c.start()
        started.extend(copies)
        return copies

    def arrive(copies):
        for c in copies:
            c.wait_recv()

    def quarter(q):
        return pl.ds(pl.multiple_of(q * fq, 128), fq)

    cot_x = begin(exchange(0, at_x, SIDE, lambda k: cot.at[:, quarter(wrap(x + k))],
                           lambda k: cotq.at[x]))

    ssb[...] = jnp.zeros_like(ssb)
    for p in range(2):
        ain_t[p] = ain[p].astype(F32).T.astype(BF16)
        for b in range(SIDE):
            lhs[p, b * rb + tb:(b + 1) * rb, :] = ain[p, b * rq:(b + 1) * rq, :]
    own_off = ((row * share) // tb) * rb + (row * share) % tb
    lhs[0, pl.ds(pl.multiple_of(own_off, 16), share), :] = tok[...]
    cotq[x] = cot[:, quarter(x)]

    def direction(p, q):
        w_copy(p, q).wait()
        left = aout[p, :, quarter(q)]
        step = min(128, depth)

        def body(i, acc):
            rows = pl.ds(pl.multiple_of(i * step, step), step)
            low = jnp.dot(ain_t[p, rows, :], left, preferred_element_type=F32)
            d = wb[p, q, rows, :].astype(F32) + low
            wb[p, q, rows, :] = d.astype(BF16)
            return acc + jnp.sum((d * d).reshape(step // 8, 8, fq), axis=0)

        acc = lax.fori_loop(0, depth // step, body, jnp.zeros((8, fq), F32))
        ssb[q, p:p + 1, :] = jnp.sum(acc, axis=0, keepdims=True)

    def product(p, q):
        res = jnp.dot(lhs[p], wb[p, q], preferred_element_type=F32).astype(BF16)
        for b in range(SIDE):
            piece = res[b * rb:(b + 1) * rb, :]
            if p == 0:
                pp[0, q, b] = piece
            else:
                pp[1, b, q] = piece

    def main_copy(p, d, kind, j):
        c1, s = first[p], wrap(second[p] + j)
        peer = ring1[p](1 if d == 0 else -1)
        if kind == FAR:
            rows = top if d == 0 else bottom
            src = pp.at[p, wrap(c1 + 2), s, rows, :]
            dst = rfar.at[p, j, rows, :]
        else:
            rows = top if (d == 0) == (kind == ACC) else bottom
            src = pp.at[p, wrap(c1 + (1 if d == 0 else -1)), s, rows, :]
            dst = rnear.at[p, d, j, rows, :]
        i = ((p * 2 + d) * 3 + kind) * SIDE + j
        return remote(src, dst, main_s.at[i], main_r.at[i], peer)

    def ph2_copy(p, d, kind):
        c1, c2 = first[p], second[p]
        peer = ring2[p](1 if d == 0 else -1)
        if kind == FAR:
            rows = top if d == 0 else bottom
            src = pp.at[p, c1, wrap(c2 + 2), rows, :]
            dst = sfar.at[p, rows, :]
        else:
            rows = top if (d == 0) == (kind == ACC) else bottom
            src = pp.at[p, c1, wrap(c2 + (1 if d == 0 else -1)), rows, :]
            dst = snear.at[p, d, rows, :]
        i = (p * 2 + d) * 3 + kind
        return remote(src, dst, ph2_s.at[i], ph2_r.at[i], peer)

    def stage(m, carry):
        j_dir = (2 - m + 3 * ((m * (m - 1)) // 2) + 8) % SIDE
        i_p = m - 2
        j_p = (2 - i_p + 3 * ((i_p * (i_p - 1)) // 2) + 8) % SIDE

        @pl.when(m == 2)
        def _():
            for i in [1, n_z - 1] + list(range(2, n_z - 1)):
                tok_copy(i).wait_recv()
                tok_copy(n_z - 1 + i).start()
            tok_copy(0).wait_recv()
            for i in range(n_z, n_tok):
                tok_copy(i).wait_recv()
            for b in range(SIDE):
                lhs[1, b * rb:b * rb + tb, :] = lhs[0, b * rb:b * rb + tb, :]

        @pl.when(m >= 2)
        def _():
            q = wrap(x + j_p)
            product(0, q)

            @pl.when(i_p == 0)
            def _():
                for j in ORDER:
                    for d in range(2):
                        main_copy(0, d, FAR, j).start()

            @pl.when(i_p == 1)
            def _():
                for j in ORDER:
                    main_copy(0, 0, RAW, j).start()

            @pl.when(i_p == 2)
            def _():
                for j in ORDER:
                    main_copy(0, 1, RAW, j).start()

            product(1, q)
            for d in range(2):
                main_copy(1, d, FAR, j_p).start()
            for d in range(2):
                main_copy(1, d, RAW, j_p).start()

        @pl.when(m < SIDE)
        def _():
            q = wrap(x + j_dir)
            for p in range(2):
                direction(p, q)

        return carry

    lax.fori_loop(0, SIDE + 2, stage, 0)

    ss_x = begin(exchange(1, at_x, SIDE, lambda k: ssb.at[wrap(x + k)], lambda k: ssr.at[k]))
    ain_all = ain[...].reshape(2 * rank, depth)
    for b in range(SIDE):
        zb[b] = nt_dot(ain_all, lhs[0, b * rb:b * rb + tb, :]).astype(BF16)
    z_y = begin(exchange(3, at_y, SIDE, lambda k: zb.at[wrap(y + k)], lambda k: zr.at[k]))

    def add_into(dst, src):
        dst[...] = (dst[...].astype(F32) + src[...].astype(F32)).astype(BF16)

    for j in ORDER:
        for p in range(2):
            for d in range(2):
                main_copy(p, d, FAR, j).wait_recv()
                rows = top if d == 0 else bottom
                near = wrap(first[p] + (1 if d == 0 else -1))
                add_into(pp.at[p, near, wrap(second[p] + j), rows, :], rfar.at[p, j, rows, :])
                main_copy(p, d, ACC, j).start()

    arrive(ss_x)
    ssx[...] = ssb[x] + ssr[1] + ssr[2] + ssr[3]
    ss_y = begin(exchange(2, at_y, SIDE, lambda k: ssx, lambda k: ssr2.at[k]))
    arrive(z_y)
    zx[...] = (zb[y].astype(F32) + zr[1].astype(F32) + zr[2].astype(F32)
               + zr[3].astype(F32)).astype(BF16)
    z_x = begin(exchange(4, at_x, SIDE, lambda k: zx, lambda k: zr2.at[k]))

    for j in ORDER:
        for p in range(2):
            for d in range(2):
                main_copy(p, d, RAW, j).wait_recv()
                main_copy(p, d, ACC, j).wait_recv()
            mine = pp.at[p, first[p], wrap(second[p] + j)]
            mine[...] = (mine[...].astype(F32) + rnear[p, 0, j].astype(F32)
                         + rnear[p, 1, j].astype(F32)).astype(BF16)
            if j == 2:
                for d in range(2):
                    ph2_copy(p, d, FAR).start()
            elif j == 1:
                ph2_copy(p, 0, RAW).start()
            elif j == 3:
                ph2_copy(p, 1, RAW).start()

    arrive(ss_y)
    total = ssx[0:2] + ssr2[1, 0:2] + ssr2[2, 0:2] + ssr2[3, 0:2]
    norm = jnp.sqrt(total + EPSILON)
    mag_q = mag[:, quarter(x)]
    coef = mag_q / norm
    arrive(z_x)
    zs[...] = (zx[...].astype(F32) + zr2[1].astype(F32) + zr2[2].astype(F32)
               + zr2[3].astype(F32)).astype(BF16)
    arrive(cot_x)

    for p in range(2):
        for d in range(2):
            ph2_copy(p, d, FAR).wait_recv()
            rows = top if d == 0 else bottom
            near = wrap(second[p] + (1 if d == 0 else -1))
            add_into(pp.at[p, first[p], near, rows, :], sfar.at[p, rows, :])
            ph2_copy(p, d, ACC).start()
    for p in range(2):
        for d in range(2):
            ph2_copy(p, d, RAW).wait_recv()
            ph2_copy(p, d, ACC).wait_recv()

    def summed(p, rows):
        return (pp[p, first[p], second[p], rows, :].astype(F32)
                + snear[p, 0, rows, :].astype(F32) + snear[p, 1, rows, :].astype(F32))

    coef0, coef1 = coef[0:1], coef[1:2]
    chunk = min(16, own_rows)
    per = own_rows // chunk

    def gating(i, carry):
        acc0, acc1 = carry
        rows = pl.ds(pl.multiple_of(i * chunk, chunk), chunk)
        inner = pl.ds(pl.multiple_of((i % per) * chunk, chunk), chunk)
        raw0, raw1 = summed(0, rows), summed(1, rows)
        gate, up = raw0 * coef0, raw1 * coef1
        sig = jax.nn.sigmoid(gate)
        hidq[i // per, inner, :] = (gate * sig * up).astype(BF16)
        c = cotq[i // per, inner, :].astype(F32)
        d0 = (c * up * sig * (1.0 + gate * (1.0 - sig))).astype(BF16)
        d1 = (c * gate * sig).astype(BF16)
        dsc[0, rows, :] = d0
        dsc[1, rows, :] = d1
        s0 = jnp.sum((d0.astype(F32) * raw0).reshape(chunk // 8, 8, fq), axis=0)
        s1 = jnp.sum((d1.astype(F32) * raw1).reshape(chunk // 8, 8, fq), axis=0)
        return (acc0 + s0, acc1 + s1)

    zero = jnp.zeros((8, fq), F32)
    acc0, acc1 = lax.fori_loop(0, tb // chunk, gating, (zero, zero))
    st[...] = zero
    st[0:1] = jnp.sum(acc0, axis=0, keepdims=True)
    st[1:2] = jnp.sum(acc1, axis=0, keepdims=True)
    st_y = begin(exchange(6, at_y, SIDE, lambda k: st, lambda k: strr.at[k]))

    for p in range(2):
        res = jnp.dot(zs[p * rank:(p + 1) * rank, :], dsc[p], preferred_element_type=F32)
        for b in range(SIDE):
            g1[b, p] = res[b * rq:(b + 1) * rq, :].astype(BF16)
    g1_y = begin(exchange(8, at_y, SIDE, lambda k: g1.at[wrap(y + k)], lambda k: g1r.at[k]))
    for p in range(2):
        scaled = (aout[p, :, quarter(x)].astype(F32) * coef[p:p + 1]).astype(BF16)
        wv[p * rank:(p + 1) * rank, :] = nt_dot(scaled, dsc[p]).astype(BF16)
    w_x = begin(exchange(9, at_x, SIDE, lambda k: wv, lambda k: wr.at[k]))
    hid_x = begin(exchange(5, at_x, SIDE, lambda k: hidq.at[wrap(x + k)], lambda k: hidr.at[x]))
    hidr[x] = hidq[x]

    arrive(st_y)
    stat = st[0:2] + strr[1, 0:2] + strr[2, 0:2] + strr[3, 0:2]
    tilt = mag_q * stat / (norm * norm * norm)
    bb[...] = zero
    bb[0:2] = tilt
    bb[2:4] = stat / norm
    b_x = begin(exchange(7, at_x, SIDE, lambda k: bb, lambda k: ball.at[x]))
    ball[x] = bb[...]

    arrive(g1_y)
    for p in range(2):
        both = (g1[y, p].astype(F32) + g1r[1, p].astype(F32) + g1r[2, p].astype(F32)
                + g1r[3, p].astype(F32))
        piece = coef[p:p + 1] * both - tilt[p:p + 1] * summed(p, pl.ds(tb, rq))
        if p == 0:
            gall0[y, x] = piece.astype(BF16)
        else:
            gall1[x, y] = piece.astype(BF16)
    ga_x = begin(exchange(11, at_x, SIDE, lambda k: gall0.at[y, x], lambda k: gall0.at[y, x]))
    gb_y = begin(exchange(13, at_y, SIDE, lambda k: gall1.at[x, y], lambda k: gall1.at[x, y]))

    arrive(w_x)
    wx[...] = (wv[...].astype(F32) + wr[1].astype(F32) + wr[2].astype(F32)
               + wr[3].astype(F32)).astype(BF16)
    w_y = begin(exchange(10, at_y, SIDE, lambda k: wx, lambda k: wall.at[y]))
    wall[y] = wx[...]

    arrive(ga_x)
    ga_y = begin(exchange(12, at_y, SIDE, lambda k: gall0.at[y], lambda k: gall0.at[y]))
    arrive(gb_y)
    gb_x = begin(exchange(14, at_x, SIDE, lambda k: gall1.at[x], lambda k: gall1.at[x]))

    arrive(b_x)
    arrive(w_y)
    out_rows = 2 * rank // n_row
    for p in range(2):
        total_in = jnp.zeros((rank, depth), F32)
        for b in range(SIDE):
            total_in = total_in + jnp.dot(
                wall[b, p * rank:(p + 1) * rank, :], lhs[0, b * rb:b * rb + tb, :],
                preferred_element_type=F32)
        for q in range(SIDE):
            scaled = (aout[p, :, q * fq:(q + 1) * fq].astype(F32) * ball[q, p:p + 1]).astype(BF16)
            total_in = total_in - nt_dot(scaled, wb[p, q])
        for b in range(rank // out_rows):
            gib[p * (rank // out_rows) + b] = total_in[b * out_rows:(b + 1) * out_rows].astype(BF16)
    gi_rs = begin(exchange(15, at_row, n_row, lambda k: gib.at[(row + k) % n_row],
                           lambda k: gir.at[k]))

    for q in range(SIDE):
        gm[:, q * fq:(q + 1) * fq] = ball[q, 2:4, :]
    arrive(hid_x)
    for q in range(SIDE):
        hid[:, q * fq:(q + 1) * fq] = hidr[q]

    arrive(gi_rs)
    acc = gib[row].astype(F32)
    for k in range(1, n_row):
        acc = acc + gir[k].astype(F32)
    gio[...] = acc.astype(BF16)
    gi_ag = begin(exchange(16, at_row, n_row, lambda k: gio, lambda k: giall.at[row]))
    giall[row] = gio[...]

    arrive(ga_y)
    arrive(gb_x)
    for q in range(SIDE):
        for b in range(SIDE):
            go[0, b * rq:(b + 1) * rq, q * fq:(q + 1) * fq] = gall0[b, q]
            go[1, b * rq:(b + 1) * rq, q * fq:(q + 1) * fq] = gall1[q, b]
    arrive(gi_ag)
    for p in range(2):
        for b in range(rank // out_rows):
            gi[p, b * out_rows:(b + 1) * out_rows, :] = giall[p * (rank // out_rows) + b]

    for i in range(n_tok):
        tok_copy(i).wait_send()
    for p in range(2):
        for d in range(2):
            for kind in range(3):
                for j in range(SIDE):
                    main_copy(p, d, kind, j).wait_send()
                ph2_copy(p, d, kind).wait_send()
    for c in started:
        c.wait_send()


def solution(mesh):
    n_row = mesh.shape["row"]

    def on_device(tokens, weights, adapter_in, adapter_out, magnitude, hidden_cot):
        share, depth = tokens.shape
        rank = adapter_in.shape[1]
        width = adapter_out.shape[2]
        fq = width // SIDE
        tb = share * n_row // SIDE
        rq = rank // SIDE
        rb = tb + rq
        own_rows = tb // SIDE
        pr = 2 * rank
        vm = pltpu.VMEM
        dma = pltpu.SemaphoreType.DMA
        scratch = [
            vm((2, SIDE * rb, depth), BF16),
            vm((2, SIDE, depth, fq), BF16),
            vm((2, SIDE, SIDE, rb, fq), BF16),
            vm((2, depth, rank), BF16),
            vm((2, SIDE, rb, fq), BF16),
            vm((2, 2, SIDE, rb, fq), BF16),
            vm((2, rb, fq), BF16),
            vm((2, 2, rb, fq), BF16),
            vm((SIDE, own_rows, fq), BF16),
            vm((SIDE, 8, fq), F32),
            vm((8, fq), F32),
            vm((SIDE, 8, fq), F32),
            vm((SIDE, 8, fq), F32),
            vm((SIDE, pr, tb), BF16),
            vm((pr, tb), BF16),
            vm((pr, tb), BF16),
            vm((SIDE, pr, tb), BF16),
            vm((SIDE, pr, tb), BF16),
            vm((SIDE, own_rows, fq), BF16),
            vm((SIDE, own_rows, fq), BF16),
            vm((2, tb, fq), BF16),
            vm((8, fq), F32),
            vm((SIDE, 8, fq), F32),
            vm((8, fq), F32),
            vm((SIDE, 8, fq), F32),
            vm((SIDE, 2, rq, fq), BF16),
            vm((SIDE, 2, rq, fq), BF16),
            vm((pr, tb), BF16),
            vm((pr, tb), BF16),
            vm((SIDE, pr, tb), BF16),
            vm((SIDE, pr, tb), BF16),
            vm((SIDE, SIDE, rq, fq), BF16),
            vm((SIDE, SIDE, rq, fq), BF16),
            vm((n_row, pr // n_row, depth), BF16),
            vm((n_row, pr // n_row, depth), BF16),
            vm((pr // n_row, depth), BF16),
            vm((n_row, pr // n_row, depth), BF16),
            dma((2 * SIDE,)),
            dma((n_row,)),
            dma((n_row,)),
            dma((12 * SIDE,)),
            dma((12 * SIDE,)),
            dma((12,)),
            dma((12,)),
            dma((EXCHANGES * 8,)),
            dma((EXCHANGES * 8,)),
        ]
        vmem = pl.BlockSpec(memory_space=pltpu.VMEM)
        hidden, grad_in, grad_out, grad_mag = pl.pallas_call(
            functools.partial(kernel, n_row),
            out_shape=(
                jax.ShapeDtypeStruct(hidden_cot.shape, BF16),
                jax.ShapeDtypeStruct(adapter_in.shape, BF16),
                jax.ShapeDtypeStruct(adapter_out.shape, BF16),
                jax.ShapeDtypeStruct(magnitude.shape, F32),
            ),
            in_specs=[vmem, pl.BlockSpec(memory_space=pl.ANY), vmem, vmem, vmem, vmem],
            out_specs=(vmem, vmem, vmem, vmem),
            scratch_shapes=scratch,
            compiler_params=pltpu.CompilerParams(
                collective_id=0, has_side_effects=True, vmem_limit_bytes=60 * 2**20
            ),
        )(tokens, weights, adapter_in, adapter_out, magnitude, hidden_cot)
        return (hidden, grad_in.astype(F32), grad_out.astype(F32), grad_mag)

    in_specs = (
        P("row", "col"),
        P(None, "col", "row"),
        P(None, None, "col"),
        P(None, None, "row"),
        P(None, "row"),
        P("col", "row"),
    )
    out_specs = (P("col", "row"), P(None, None, "col"), P(None, None, "row"), P(None, "row"))
    return jax.shard_map(
        on_device, mesh=mesh, in_specs=in_specs, out_specs=out_specs, check_vma=False
    )
```

time: 456 us -> 101 us (0.22)
  waiting for transfers between devices: 229 us -> 0 us
  blocking collectives: 152 us -> 0 us
  Pallas kernels: 0 us -> 93.1 us
  matrix products: 26.5 us -> 0 us
  local copies, waits for them, and re-layouts: 24 us -> 3 us
  between operations: 14.6 us -> 0.64 us
    psum x2 -> x0, waiting for transfers between devices: 161 us -> none  [the longest x1 87.2 us: on_device(): lax.psum((coef[:, None, :] * first - coef_dir[:, None, :] * second).astyp...]
    psum x2 -> x0, blocking collectives: 121 us -> none  [the longest x1 62.4 us: on_device(): square_sum = lax.psum(jnp.sum(direction * direction, axis=1), 'col')]
    pallas_call x0 -> x1, Pallas kernels: none -> 93.1 us  [on_device(): pl.pallas_call(functools.partial(kernel, n_row), out_shape=(jax.ShapeDtyp...]
    unnamed x5 -> x0, waiting for transfers between devices: 67.8 us -> none
    all_gather x2 -> x0, blocking collectives: 31.6 us -> none  [the longest x1 15.9 us: on_device(): token_all = lax.all_gather(tokens, 'row', axis=0, tiled=True)]
    dot_general x8 -> x0, matrix products: 26.5 us -> none  [the longest x1 6.2 us: on_device(): jnp.einsum('td,pdf->ptf', token_all, direction_b, preferred_element_type=...]
    convert_element_type x1 -> x0, local copies, waits for them, and re-layouts: 19 us -> none  [on_device(): partial_value.astype(BF16)]
  transfers between devices with their start and end apart: 4 -> 0, of which waited for: 3 -> 0; matrix products, arithmetic and copies ran while one was open for 5% -> 0% of each run, Pallas kernels for 0% -> 0%
where the time goes in v2:
time: 101 us
  Pallas kernels  93.1 us (92%)
  other arithmetic  4.22 us (4%)
  local copies, waits for them, and re-layouts  3 us (3%)
    pallas_call x1, Pallas kernels, on_device(): pl.pallas_call(functools.partial(kernel, n_row), out_shape=(jax.ShapeDtyp...  93.1 us
    convert_element_type x2, other arithmetic, on_device(): return (hidden, grad_in.astype(F32), grad_out.astype(F32), grad_mag)  4.22 us
    unnamed x2, local copies, waits for them, and re-layouts  3 us

profile of v2, /device:TPU:1, one launch (start us, length us, event | category | flops | bytes accessed | tf_op | source)
XLA Modules:
  0.0 100.9 jit_solution(15214588367632007606)
XLA Ops:
  0.6 93.1 %shard_map.93 = (bf16[32,3584]{1,0:T(8,128)(2,1)}, bf16[2,64,512]{2,1,0:T(8,128)(2,1)}, bf16[2,64,3584]{2,1,0:T(8,128)(2,1)}, f32[2,3584]{1,0:T(2,128)}) custom-call(bf16[64,512]{1,0:T(8,128)(2,1)} %tok.1, bf16[2,512,3584]{2,1,0:T(8,128)(2,1)} %w_hbm.1, bf16[2,64,512]{2,1,0:T(8,128)(2,1)} %ain.1, bf16[2,64,3584]{2,1,0:T(8,128)(2,1)} %aout.1, f32[2,3584]{1,0:T(2,128)} %mag.1, ...), custom_call_target="tpu_custom_call" | custom-call | tf_op jit(solution)/shard_map/pallas_call | solution.py:499
  93.7 2.6 %convert_element_type.7 = f32[2,64,3584]{2,1,0:T(8,128)} convert(bf16[2,64,3584]{2,1,0:T(8,128)(2,1)} %get-tuple-element.10) | non-fusion elementwise | flops 458752 | bytes 2752512 | tf_op jit(solution)/shard_map/convert_element_type | solution.py:514
  96.3 1.6 %convert_element_type.6 = f32[2,64,512]{2,1,0:T(8,128)} convert(bf16[2,64,512]{2,1,0:T(8,128)(2,1)} %get-tuple-element.9) | non-fusion elementwise | flops 65536 | bytes 393216 | tf_op jit(solution)/shard_map/convert_element_type | solution.py:514
  97.9 1.6 %copy.12 = bf16[32,3584]{1,0:T(8,128)(2,1)} copy(bf16[32,3584]{1,0:T(8,128)(2,1)} %get-tuple-element.16) | data formatting | bytes 458752
  99.6 1.4 %copy.13 = f32[2,3584]{1,0:T(2,128)} copy(f32[2,3584]{1,0:T(2,128)} %get-tuple-element.19) | data formatting | bytes 57344

commit v3 on v2

v3 whole, which is shorter than its diff:
```python
import functools

import jax
import jax.numpy as jnp
from jax import lax
from jax.experimental import pallas as pl
from jax.experimental.pallas import tpu as pltpu
from jax.sharding import PartitionSpec as P

EPSILON = 1e-06
F32 = jnp.float32
BF16 = jnp.bfloat16
MESH = pl.DeviceIdType.MESH
SIDE = 4
ORDER = (2, 1, 3, 0)
EXCHANGES = 19
FAR, RAW, ACC = 0, 1, 2


def nt_dot(a, b):
    return lax.dot_general(a, b, (((1,), (1,)), ((), ())), preferred_element_type=F32)


def kernel(n_row, tok, w_hbm, ain, aout, mag, cot, hid_out, gi_out, go_out, gm_out,
           lhs, wb, pp, ainv, aoutv, magv, ain_t, rfar, rnear, sfar, snear, cotq, ssb, ssx, ssr, ssr2,
           zb, zx, zs, zr, zr2, hidq, hidr, dsc, st, strr, bb, ball, gmq, g1, g1r,
           wv, wx, wr, wall, qq, qr, qx, qr2, gall, gib, gir, gio, giall, tin,
           w_sem, in_sem, out_sem, tok_s, tok_r, main_s, main_r, ph2_s, ph2_r, q_s, q_r, ex_s, ex_r):
    row, col = lax.axis_index("row"), lax.axis_index("col")
    y, x = col // SIDE, col % SIDE
    n_z = n_row // 2
    z, core = row // 2, row % 2
    share, depth = tok.shape
    rank = ain.shape[1]
    width = aout.shape[2]
    fq = width // SIDE
    tb = share * n_row // SIDE
    rq = rank // SIDE
    own_rows = tb // SIDE
    half = tb // 2
    top, bottom = pl.ds(0, half), pl.ds(half, half)
    first, second = (x, y), (y, x)

    def wrap(v):
        return (v + 2 * SIDE) % SIDE

    def at_x(k):
        return (row, y * SIDE + wrap(x + k))

    def at_y(k):
        return (row, wrap(y + k) * SIDE + x)

    def at_row(k):
        return ((row + k) % n_row, col)

    def at_core():
        return (z * 2 + (1 - core), col)

    def at_z(k):
        return (((z + k) % n_z) * 2 + core, col)

    ring1 = (at_x, at_y)
    ring2 = (at_y, at_x)

    def quarter(q):
        return pl.ds(pl.multiple_of(q * fq, 128), fq)

    def offset(m):
        return (2 - m + 3 * ((m * (m - 1)) // 2) + 8) % SIDE

    barrier = pltpu.get_barrier_semaphore()
    peers = [at_x(k) for k in (1, 2, 3)] + [at_y(k) for k in (1, 2, 3)]
    peers += [at_row(k) for k in range(1, n_row)]
    for peer in peers:
        pl.semaphore_signal(barrier, inc=1, device_id=peer, device_id_type=MESH)

    def own_tokens():
        return lhs.at[pl.ds(pl.multiple_of(row * share, 16), share), :]

    loads = [
        pltpu.make_async_copy(ain, ainv, in_sem.at[0]),
        pltpu.make_async_copy(aout, aoutv, in_sem.at[1]),
        pltpu.make_async_copy(tok, own_tokens(), in_sem.at[2]),
        pltpu.make_async_copy(mag, magv, in_sem.at[3]),
        pltpu.make_async_copy(cot.at[:, quarter(x)], cotq.at[x], in_sem.at[4]),
    ]

    def w_copy(p, q):
        return pltpu.make_async_copy(
            w_hbm.at[p, :, quarter(q)], wb.at[p, q], w_sem.at[p * SIDE + q])

    loads[0].start()
    loads[1].start()
    for p in range(2):
        w_copy(p, wrap(x + ORDER[0])).start()
    for c in loads[2:]:
        c.start()
    for j in ORDER[1:]:
        for p in range(2):
            w_copy(p, wrap(x + j)).start()

    def remote(src, dst, send, recv, peer):
        return pltpu.make_async_remote_copy(
            src_ref=src, dst_ref=dst, send_sem=send, recv_sem=recv,
            device_id=peer, device_id_type=MESH)

    def tok_rows(owner):
        return lhs.at[pl.ds(pl.multiple_of(owner * share, 16), share), :]

    def tok_copy(i):
        if i == 0:
            owner, peer = row, at_core()
        elif i < n_z:
            owner, peer = row, at_z(i)
        else:
            owner = ((z + n_z - (i - n_z + 1)) % n_z) * 2 + core
            peer = at_core()
        return remote(tok_rows(owner), tok_rows(owner), tok_s.at[i], tok_r.at[i], peer)

    n_tok = 2 * n_z - 1
    z_order = [1, n_z - 1] + list(range(2, n_z - 1))

    def exchange(e, peer_of, count, src, dst):
        return [remote(src(k), dst(k), ex_s.at[e * 8 + k], ex_r.at[e * 8 + k], peer_of(k))
                for k in range(1, count)]

    started = []

    def begin(copies):
        for c in copies:
            c.start()
        started.extend(copies)
        return copies

    def arrive(copies):
        for c in copies:
            c.wait_recv()

    def q_first(p, k, j):
        if p == 0:
            src, dst, i = qq.at[0, wrap(x + k)], qr.at[0, k], k
        else:
            q = wrap(x + j)
            src, dst, i = qq.at[1, wrap(y + k), q], qr.at[1, k, q], SIDE + k * SIDE + j
        return remote(src, dst, q_s.at[i], q_r.at[i], ring1[p](k))

    for i in range(2):
        loads[i].wait()
    for p in range(2):
        ain_t[p] = ainv[p].astype(F32).T.astype(BF16)
    step = min(128, depth)

    def prepare(m):
        q = wrap(x + offset(m))
        for p in range(2):
            w_copy(p, q).wait()
            left = aoutv[p, :, quarter(q)]

            def body(i, acc):
                rows = pl.ds(pl.multiple_of(i * step, step), step)
                low = jnp.dot(ain_t[p, rows, :], left, preferred_element_type=F32)
                d = wb[p, q, rows, :].astype(F32) + low
                wb[p, q, rows, :] = d.astype(BF16)
                return acc + jnp.sum((d * d).reshape(step // 8, 8, fq), axis=0)

            acc = lax.fori_loop(0, depth // step, body, jnp.zeros((8, fq), F32))
            ssb[q, p:p + 1, :] = jnp.sum(acc, axis=0, keepdims=True)
            res = jnp.dot(ainv[p], wb[p, q], preferred_element_type=F32).astype(BF16)
            for b in range(SIDE):
                piece = res[b * rq:(b + 1) * rq, :]
                if p == 0:
                    qq[0, q, b] = piece
                else:
                    qq[1, b, q] = piece

    def q_send(m):
        j = offset(m)

        @pl.when(m < SIDE - 1)
        def _():
            q_first(0, j, 0).start()

        for k in (2, 1, 3):
            q_first(1, k, j).start()

    def early(m, carry):
        prepare(m)
        return carry

    lax.fori_loop(0, 2, early, 0)

    pl.semaphore_wait(barrier, len(peers))
    loads[2].wait()
    for i in z_order + [0]:
        tok_copy(i).start()
    cot_x = begin(exchange(0, at_x, SIDE, lambda k: cot.at[:, quarter(wrap(x + k))],
                           lambda k: cotq.at[x]))

    def early_send(m, carry):
        q_send(m)
        return carry

    lax.fori_loop(0, 2, early_send, 0)

    def later(m, carry):
        prepare(m)
        q_send(m)
        return carry

    lax.fori_loop(2, SIDE, later, 0)
    ss_x = begin(exchange(1, at_x, SIDE, lambda k: ssb.at[wrap(x + k)], lambda k: ssr.at[k]))

    for i in z_order:
        tok_copy(i).wait_recv()
        tok_copy(n_z - 1 + i).start()
    tok_copy(0).wait_recv()
    for i in range(n_z, n_tok):
        tok_copy(i).wait_recv()

    def product(p, q):
        res = jnp.dot(lhs[...], wb[p, q], preferred_element_type=F32).astype(BF16)
        for b in range(SIDE):
            piece = res[b * tb:(b + 1) * tb, :]
            if p == 0:
                pp[0, q, b] = piece
            else:
                pp[1, b, q] = piece

    def main_copy(p, d, kind, j):
        c1, s = first[p], wrap(second[p] + j)
        peer = ring1[p](1 if d == 0 else -1)
        if kind == FAR:
            rows = top if d == 0 else bottom
            src = pp.at[p, wrap(c1 + 2), s, rows, :]
            dst = rfar.at[p, j, rows, :]
        else:
            rows = top if (d == 0) == (kind == ACC) else bottom
            src = pp.at[p, wrap(c1 + (1 if d == 0 else -1)), s, rows, :]
            dst = rnear.at[p, d, j, rows, :]
        i = ((p * 2 + d) * 3 + kind) * SIDE + j
        return remote(src, dst, main_s.at[i], main_r.at[i], peer)

    def ph2_copy(p, d, kind):
        c1, c2 = first[p], second[p]
        peer = ring2[p](1 if d == 0 else -1)
        if kind == FAR:
            rows = top if d == 0 else bottom
            src = pp.at[p, c1, wrap(c2 + 2), rows, :]
            dst = sfar.at[p, rows, :]
        else:
            rows = top if (d == 0) == (kind == ACC) else bottom
            src = pp.at[p, c1, wrap(c2 + (1 if d == 0 else -1)), rows, :]
            dst = snear.at[p, d, rows, :]
        i = (p * 2 + d) * 3 + kind
        return remote(src, dst, ph2_s.at[i], ph2_r.at[i], peer)

    z_y = exchange(3, at_y, SIDE, lambda k: zb.at[wrap(y + k)], lambda k: zr.at[k])

    def stage(i_p, carry):
        j_p = offset(i_p)
        q = wrap(x + j_p)
        product(0, q)

        @pl.when(i_p == 0)
        def _():
            for j in ORDER:
                for d in range(2):
                    main_copy(0, d, FAR, j).start()

        @pl.when(i_p == 1)
        def _():
            for j in ORDER[:3]:
                main_copy(0, 0, RAW, j).start()

        @pl.when(i_p == 2)
        def _():
            for j in ORDER[:3]:
                main_copy(0, 1, RAW, j).start()

        product(1, q)
        for d in range(2):
            main_copy(1, d, FAR, j_p).start()

        @pl.when(i_p < 3)
        def _():
            for d in range(2):
                main_copy(1, d, RAW, j_p).start()

        @pl.when(i_p == 0)
        def _():
            ain_all = ainv[...].reshape(2 * rank, depth)
            for b in range(SIDE):
                zb[b] = nt_dot(ain_all, lhs[b * tb:(b + 1) * tb, :]).astype(BF16)
            for c in z_y:
                c.start()

        return carry

    lax.fori_loop(0, SIDE, stage, 0)

    def add_into(dst, src):
        dst[...] = (dst[...].astype(F32) + src[...].astype(F32)).astype(BF16)

    def accumulate(j):
        for p in range(2):
            for d in range(2):
                main_copy(p, d, FAR, j).wait_recv()
                rows = top if d == 0 else bottom
                near = wrap(first[p] + (1 if d == 0 else -1))
                add_into(pp.at[p, near, wrap(second[p] + j), rows, :], rfar.at[p, j, rows, :])

    for j in ORDER[:3]:
        accumulate(j)
        for p in range(2):
            for d in range(2):
                main_copy(p, d, ACC, j).start()

    arrive(ss_x)
    ssx[...] = ssb[x] + ssr[1] + ssr[2] + ssr[3]
    ss_y = begin(exchange(2, at_y, SIDE, lambda k: ssx, lambda k: ssr2.at[k]))
    arrive(z_y)
    zx[...] = (zb[y].astype(F32) + zr[1].astype(F32) + zr[2].astype(F32)
               + zr[3].astype(F32)).astype(BF16)
    z_x = begin(exchange(4, at_x, SIDE, lambda k: zx, lambda k: zr2.at[k]))
    for k in (2, 1, 3):
        q_first(0, k, 0).wait_recv()
    for j in ORDER:
        for k in (2, 1, 3):
            q_first(1, k, j).wait_recv()
    q_two = []
    for p in range(2):
        qx[p] = (qq[p, first[p]].astype(F32) + qr[p, 1].astype(F32) + qr[p, 2].astype(F32)
                 + qr[p, 3].astype(F32)).astype(BF16)
        q_two.append(begin(exchange(
            17 + p, ring2[p], SIDE, lambda k, p=p: qx.at[p, wrap(second[p] + k)],
            lambda k, p=p: qr2.at[p, k])))

    def finish(j):
        for p in range(2):
            for d in range(2):
                main_copy(p, d, RAW, j).wait_recv()
                main_copy(p, d, ACC, j).wait_recv()
            mine = pp.at[p, first[p], wrap(second[p] + j)]
            mine[...] = (mine[...].astype(F32) + rnear[p, 0, j].astype(F32)
                         + rnear[p, 1, j].astype(F32)).astype(BF16)

    finish(2)
    for p in range(2):
        for d in range(2):
            ph2_copy(p, d, FAR).start()
    finish(1)
    for p in range(2):
        ph2_copy(p, 0, RAW).start()
    finish(3)
    for p in range(2):
        ph2_copy(p, 1, RAW).start()
    for p in range(2):
        for d in range(2):
            main_copy(p, d, RAW, 0).start()
    accumulate(0)
    for p in range(2):
        for d in range(2):
            ph2_copy(p, d, FAR).wait_recv()
            rows = top if d == 0 else bottom
            near = wrap(second[p] + (1 if d == 0 else -1))
            add_into(pp.at[p, first[p], near, rows, :], sfar.at[p, rows, :])
            ph2_copy(p, d, ACC).start()
    for p in range(2):
        for d in range(2):
            main_copy(p, d, ACC, 0).start()
    arrive(ss_y)
    total = ssx[...] + ssr2[1] + ssr2[2] + ssr2[3]
    norm = jnp.sqrt(total + EPSILON)
    loads[3].wait()
    mag_q = magv[:, quarter(x)]
    coef = mag_q / norm
    arrive(z_x)
    zs[...] = (zx[...].astype(F32) + zr2[1].astype(F32) + zr2[2].astype(F32)
               + zr2[3].astype(F32)).astype(BF16)
    arrive(cot_x)
    loads[4].wait()

    finish(0)
    for p in range(2):
        for d in range(2):
            ph2_copy(p, d, RAW).wait_recv()
            ph2_copy(p, d, ACC).wait_recv()

    def summed(p, rows):
        return (pp[p, first[p], second[p], rows, :].astype(F32)
                + snear[p, 0, rows, :].astype(F32) + snear[p, 1, rows, :].astype(F32))

    coef0, coef1 = coef[0:1], coef[1:2]
    chunk = min(16, own_rows)
    per = own_rows // chunk

    def gating(i, carry):
        acc0, acc1 = carry
        rows = pl.ds(pl.multiple_of(i * chunk, chunk), chunk)
        inner = pl.ds(pl.multiple_of((i % per) * chunk, chunk), chunk)
        raw0, raw1 = summed(0, rows), summed(1, rows)
        gate, up = raw0 * coef0, raw1 * coef1
        sig = jax.nn.sigmoid(gate)
        hidq[i // per, inner, :] = (gate * sig * up).astype(BF16)
        c = cotq[i // per, inner, :].astype(F32)
        d0 = (c * up * sig * (1.0 + gate * (1.0 - sig))).astype(BF16)
        d1 = (c * gate * sig).astype(BF16)
        dsc[0, rows, :] = d0
        dsc[1, rows, :] = d1
        s0 = jnp.sum((d0.astype(F32) * raw0).reshape(chunk // 8, 8, fq), axis=0)
        s1 = jnp.sum((d1.astype(F32) * raw1).reshape(chunk // 8, 8, fq), axis=0)
        return (acc0 + s0, acc1 + s1)

    zero = jnp.zeros((8, fq), F32)
    acc0, acc1 = lax.fori_loop(0, tb // chunk, gating, (zero, zero))
    st[0:1] = jnp.sum(acc0, axis=0, keepdims=True)
    st[1:2] = jnp.sum(acc1, axis=0, keepdims=True)
    st_y = begin(exchange(6, at_y, SIDE, lambda k: st, lambda k: strr.at[k]))

    for p in range(2):
        scaled = (aoutv[p, :, quarter(x)].astype(F32) * coef[p:p + 1]).astype(BF16)
        wv[p * rank:(p + 1) * rank, :] = nt_dot(scaled, dsc[p]).astype(BF16)
    w_x = begin(exchange(9, at_x, SIDE, lambda k: wv, lambda k: wr.at[k]))
    for p in range(2):
        res = jnp.dot(zs[p * rank:(p + 1) * rank, :], dsc[p], preferred_element_type=F32)
        for b in range(SIDE):
            g1[b, p] = res[b * rq:(b + 1) * rq, :].astype(BF16)
    g1_y = begin(exchange(8, at_y, SIDE, lambda k: g1.at[wrap(y + k)], lambda k: g1r.at[k]))
    hid_x = begin(exchange(5, at_x, SIDE, lambda k: hidq.at[wrap(x + k)], lambda k: hidr.at[x]))
    hidr[x] = hidq[x]

    arrive(st_y)
    stat = st[...] + strr[1] + strr[2] + strr[3]
    tilt = mag_q * stat / (norm * norm * norm)
    bb[0:2] = tilt
    bb[2:4] = stat / norm
    b_x = begin(exchange(7, at_x, SIDE, lambda k: bb, lambda k: ball.at[x]))
    ball[x] = bb[...]

    arrive(w_x)
    wx[...] = (wv[...].astype(F32) + wr[1].astype(F32) + wr[2].astype(F32)
               + wr[3].astype(F32)).astype(BF16)
    w_y = begin(exchange(10, at_y, SIDE, lambda k: wx, lambda k: wall.at[y]))
    wall[y] = wx[...]

    arrive(g1_y)
    for p in range(2):
        arrive(q_two[p])
        both = (g1[y, p].astype(F32) + g1r[1, p].astype(F32) + g1r[2, p].astype(F32)
                + g1r[3, p].astype(F32))
        low = (qx[p, second[p]].astype(F32) + qr2[p, 1].astype(F32) + qr2[p, 2].astype(F32)
               + qr2[p, 3].astype(F32))
        gall[p, second[p], first[p]] = (coef[p:p + 1] * both - tilt[p:p + 1] * low).astype(BF16)
    ga_x = begin(exchange(11, at_x, SIDE, lambda k: gall.at[0, y, x], lambda k: gall.at[0, y, x]))
    gb_y = begin(exchange(13, at_y, SIDE, lambda k: gall.at[1, x, y], lambda k: gall.at[1, x, y]))

    def tilted(p, q, b):
        scaled = (aoutv[p, :, quarter(q)].astype(F32) * b).astype(BF16)
        return nt_dot(scaled, wb[p, q])

    for p in range(2):
        tin[p] = -tilted(p, x, tilt[p:p + 1])

    arrive(w_y)
    for p in range(2):
        t1 = tin[p]
        for b in range(SIDE):
            t1 = t1 + jnp.dot(wall[b, p * rank:(p + 1) * rank, :], lhs[b * tb:(b + 1) * tb, :],
                              preferred_element_type=F32)
        tin[p] = t1

    arrive(b_x)
    out_rows = 2 * rank // n_row
    for p in range(2):
        t1 = tin[p]
        for k in range(1, SIDE):
            q = wrap(x + k)
            t1 = t1 - tilted(p, q, ball[q, p:p + 1])
        for b in range(rank // out_rows):
            gib[p * (rank // out_rows) + b] = t1[b * out_rows:(b + 1) * out_rows].astype(BF16)
    gi_rs = begin(exchange(15, at_row, n_row, lambda k: gib.at[(row + k) % n_row],
                           lambda k: gir.at[k]))

    arrive(ga_x)
    ga_y = begin(exchange(12, at_y, SIDE, lambda k: gall.at[0, y], lambda k: gall.at[0, y]))
    arrive(gb_y)
    gb_x = begin(exchange(14, at_x, SIDE, lambda k: gall.at[1, x], lambda k: gall.at[1, x]))
    for q in range(SIDE):
        gmq[q] = ball[q, 2:4, :]
    arrive(hid_x)
    outs = [
        pltpu.make_async_copy(gmq, gm_out, out_sem.at[0]),
        pltpu.make_async_copy(hidr, hid_out, out_sem.at[1]),
        pltpu.make_async_copy(gall, go_out, out_sem.at[2]),
        pltpu.make_async_copy(giall, gi_out, out_sem.at[3]),
    ]
    outs[0].start()
    outs[1].start()

    arrive(gi_rs)
    acc = gib[row].astype(F32)
    for k in range(1, n_row):
        acc = acc + gir[k].astype(F32)
    gio[...] = acc.astype(BF16)
    gi_ag = begin(exchange(16, at_row, n_row, lambda k: gio, lambda k: giall.at[row]))
    giall[row] = gio[...]

    arrive(ga_y)
    arrive(gb_x)
    outs[2].start()
    arrive(gi_ag)
    outs[3].start()

    for i in range(n_tok):
        tok_copy(i).wait_send()
    for c in z_y:
        c.wait_send()
    for k in (1, 2, 3):
        q_first(0, k, 0).wait_send()
        for j in range(SIDE):
            q_first(1, k, j).wait_send()
    for p in range(2):
        for d in range(2):
            for kind in range(3):
                for j in range(SIDE):
                    main_copy(p, d, kind, j).wait_send()
                ph2_copy(p, d, kind).wait_send()
    for c in started:
        c.wait_send()
    for c in outs:
        c.wait()


def finish_kernel(hidr, giall, gall, gmq, hid, gi, go, gm):
    fq = hidr.shape[2]
    rq = gall.shape[3]
    n_row, out_rows = giall.shape[:2]
    per = n_row // 2
    for q in range(SIDE):
        lanes = slice(q * fq, (q + 1) * fq)
        hid[:, lanes] = hidr[q]
        gm[:, lanes] = gmq[q]
        for b in range(SIDE):
            go[0, b * rq:(b + 1) * rq, lanes] = gall[0, b, q].astype(F32)
            go[1, b * rq:(b + 1) * rq, lanes] = gall[1, q, b].astype(F32)
    for p in range(2):
        for b in range(per):
            gi[p, b * out_rows:(b + 1) * out_rows, :] = giall[p * per + b].astype(F32)


def solution(mesh):
    n_row = mesh.shape["row"]

    def on_device(tokens, weights, adapter_in, adapter_out, magnitude, hidden_cot):
        share, depth = tokens.shape
        rank = adapter_in.shape[1]
        width = adapter_out.shape[2]
        fq = width // SIDE
        tb = share * n_row // SIDE
        rq = rank // SIDE
        own_rows = tb // SIDE
        pr = 2 * rank
        vm = pltpu.VMEM
        dma = pltpu.SemaphoreType.DMA
        scratch = [
            vm((SIDE * tb, depth), BF16),
            vm((2, SIDE, depth, fq), BF16),
            vm((2, SIDE, SIDE, tb, fq), BF16),
            vm((2, rank, depth), BF16),
            vm((2, rank, width), BF16),
            vm((2, width), F32),
            vm((2, depth, rank), BF16),
            vm((2, SIDE, tb, fq), BF16),
            vm((2, 2, SIDE, tb, fq), BF16),
            vm((2, tb, fq), BF16),
            vm((2, 2, tb, fq), BF16),
            vm((SIDE, own_rows, fq), BF16),
            vm((SIDE, 2, fq), F32),
            vm((2, fq), F32),
            vm((SIDE, 2, fq), F32),
            vm((SIDE, 2, fq), F32),
            vm((SIDE, pr, tb), BF16),
            vm((pr, tb), BF16),
            vm((pr, tb), BF16),
            vm((SIDE, pr, tb), BF16),
            vm((SIDE, pr, tb), BF16),
            vm((SIDE, own_rows, fq), BF16),
            vm((SIDE, own_rows, fq), BF16),
            vm((2, tb, fq), BF16),
            vm((2, fq), F32),
            vm((SIDE, 2, fq), F32),
            vm((4, fq), F32),
            vm((SIDE, 4, fq), F32),
            vm((SIDE, 2, fq), F32),
            vm((SIDE, 2, rq, fq), BF16),
            vm((SIDE, 2, rq, fq), BF16),
            vm((pr, tb), BF16),
            vm((pr, tb), BF16),
            vm((SIDE, pr, tb), BF16),
            vm((SIDE, pr, tb), BF16),
            vm((2, SIDE, SIDE, rq, fq), BF16),
            vm((2, SIDE, SIDE, rq, fq), BF16),
            vm((2, SIDE, rq, fq), BF16),
            vm((2, SIDE, rq, fq), BF16),
            vm((2, SIDE, SIDE, rq, fq), BF16),
            vm((n_row, pr // n_row, depth), BF16),
            vm((n_row, pr // n_row, depth), BF16),
            vm((pr // n_row, depth), BF16),
            vm((n_row, pr // n_row, depth), BF16),
            vm((2, rank, depth), F32),
            dma((2 * SIDE,)),
            dma((5,)),
            dma((4,)),
            dma((n_row,)),
            dma((n_row,)),
            dma((12 * SIDE,)),
            dma((12 * SIDE,)),
            dma((12,)),
            dma((12,)),
            dma((5 * SIDE,)),
            dma((5 * SIDE,)),
            dma((EXCHANGES * 8,)),
            dma((EXCHANGES * 8,)),
        ]
        anywhere = pl.BlockSpec(memory_space=pl.ANY)
        parts = pl.pallas_call(
            functools.partial(kernel, n_row),
            out_shape=(
                jax.ShapeDtypeStruct((SIDE, own_rows, fq), BF16),
                jax.ShapeDtypeStruct((n_row, pr // n_row, depth), BF16),
                jax.ShapeDtypeStruct((2, SIDE, SIDE, rq, fq), BF16),
                jax.ShapeDtypeStruct((SIDE, 2, fq), F32),
            ),
            in_specs=[anywhere] * 6,
            out_specs=(anywhere,) * 4,
            scratch_shapes=scratch,
            compiler_params=pltpu.CompilerParams(
                collective_id=0, has_side_effects=True, vmem_limit_bytes=67_043_328
            ),
        )(tokens, weights, adapter_in, adapter_out, magnitude, hidden_cot)
        return pl.pallas_call(
            finish_kernel,
            out_shape=(
                jax.ShapeDtypeStruct(hidden_cot.shape, BF16),
                jax.ShapeDtypeStruct(adapter_in.shape, F32),
                jax.ShapeDtypeStruct(adapter_out.shape, F32),
                jax.ShapeDtypeStruct(magnitude.shape, F32),
            ),
        )(*parts)

    in_specs = (
        P("row", "col"),
        P(None, "col", "row"),
        P(None, None, "col"),
        P(None, None, "row"),
        P(None, "row"),
        P("col", "row"),
    )
    out_specs = (P("col", "row"), P(None, None, "col"), P(None, None, "row"), P(None, "row"))
    return jax.shard_map(
        on_device, mesh=mesh, in_specs=in_specs, out_specs=out_specs, check_vma=False
    )
```

time: 101 us -> 91.4 us (0.905)
  other arithmetic: 4.22 us -> 0 us
  local copies, waits for them, and re-layouts: 3 us -> 0 us
  Pallas kernels: 93.1 us -> 90.6 us
    pallas_call x1, Pallas kernels: 93.1 us -> 87.8 us  [on_device(): pl.pallas_call(functools.partial(kernel, n_row), out_shape=(jax.ShapeDtyp...]
    convert_element_type x2 -> x0, other arithmetic: 4.22 us -> none  [on_device(): return (hidden, grad_in.astype(F32), grad_out.astype(F32), grad_mag)]
    unnamed x2 -> x0, local copies, waits for them, and re-layouts: 3 us -> none
    pallas_call x0 -> x1, Pallas kernels: none -> 2.8 us  [on_device(): pl.pallas_call(finish_kernel, out_shape=(jax.ShapeDtypeStruct(hidden_cot....]
where the time goes in v3:
time: 91.4 us; the launch traced here: 91.3 us
  Pallas kernels  90.6 us (99%)
    pallas_call x1, Pallas kernels, on_device(): pl.pallas_call(functools.partial(kernel, n_row), out_shape=(jax.ShapeDtyp...  87.8 us
    pallas_call x1, Pallas kernels, on_device(): pl.pallas_call(finish_kernel, out_shape=(jax.ShapeDtypeStruct(hidden_cot....  2.8 us

profile of v3, /device:TPU:1, one launch (start us, length us, event | category | flops | bytes accessed | tf_op | source)
XLA Modules:
  0.0 91.3 jit_solution(11966064093201760520)
XLA Ops:
  0.6 87.8 %shard_map.93 = (bf16[4,32,896]{2,1,0:T(8,128)(2,1)}, bf16[8,16,512]{2,1,0:T(8,128)(2,1)}, bf16[2,4,4,16,896]{4,3,2,1,0:T(8,128)(2,1)}, f32[4,2,896]{2,1,0:T(2,128)}) custom-call(bf16[64,512]{1,0:T(8,128)(2,1)} %tok.1, bf16[2,512,3584]{2,1,0:T(8,128)(2,1)} %w_hbm.1, bf16[2,64,512]{2,1,0:T(8,128)(2,1)} %ain.1, bf16[2,64,3584]{2,1,0:T(8,128)(2,1)} %aout.1, ...), custom_call_target="tpu_custom_call" | custom-call | tf_op jit(solution)/shard_map/pallas_call | solution.py:626
  88.4 2.8 %shard_map.94 = (bf16[32,3584]{1,0:T(8,128)(2,1)}, f32[2,64,512]{2,1,0:T(8,128)}, f32[2,64,3584]{2,1,0:T(8,128)}, f32[2,3584]{1,0:T(2,128)}) custom-call(bf16[4,32,896]{2,1,0:T(8,128)(2,1)} %get-tuple-element.8.hidr, bf16[8,16,512]{2,1,0:T(8,128)(2,1)} %get-tuple-element.9.giall, bf16[2,4,4,16,896]{4,3,2,1,0:T(8,128)(2,1)} %get-tuple-element.10.gall, ...), custom_call_target="tpu_custom_call" | custom-call | tf_op jit(solution)/shard_map/pallas_call | solution.py:641

commit v4 on v3

--- a/solution.py
+++ b/solution.py
@@ -25,7 +25,7 @@
            lhs, wb, pp, ainv, aoutv, magv, ain_t, rfar, rnear, sfar, snear, cotq, ssb, ssx, ssr, ssr2,
            zb, zx, zs, zr, zr2, hidq, hidr, dsc, st, strr, bb, ball, gmq, g1, g1r,
            wv, wx, wr, wall, qq, qr, qx, qr2, gall, gib, gir, gio, giall, tin,
-           w_sem, in_sem, out_sem, tok_s, tok_r, main_s, main_r, ph2_s, ph2_r, q_s, q_r, ex_s, ex_r):
+           w_sem, a_sem, in_sem, out_sem, hid_sem, gat_s, gat_r, tok_s, tok_r, main_s, main_r, ph2_s, ph2_r, q_s, q_r, ex_s, ex_r):
     row, col = lax.axis_index("row"), lax.axis_index("col")
     y, x = col // SIDE, col % SIDE
     n_z = n_row // 2
@@ -79,25 +79,27 @@
 
     loads = [
         pltpu.make_async_copy(ain, ainv, in_sem.at[0]),
-        pltpu.make_async_copy(aout, aoutv, in_sem.at[1]),
-        pltpu.make_async_copy(tok, own_tokens(), in_sem.at[2]),
-        pltpu.make_async_copy(mag, magv, in_sem.at[3]),
-        pltpu.make_async_copy(cot.at[:, quarter(x)], cotq.at[x], in_sem.at[4]),
+        pltpu.make_async_copy(tok, own_tokens(), in_sem.at[1]),
+        pltpu.make_async_copy(mag, magv, in_sem.at[2]),
+        pltpu.make_async_copy(cot.at[:, quarter(x)], cotq.at[x], in_sem.at[3]),
     ]
 
     def w_copy(p, q):
         return pltpu.make_async_copy(
             w_hbm.at[p, :, quarter(q)], wb.at[p, q], w_sem.at[p * SIDE + q])
 
+    def out_copy(q):
+        return pltpu.make_async_copy(aout.at[:, :, quarter(q)], aoutv.at[q], a_sem.at[q])
+
+    loads[1].start()
     loads[0].start()
-    loads[1].start()
-    for p in range(2):
-        w_copy(p, wrap(x + ORDER[0])).start()
-    for c in loads[2:]:
-        c.start()
-    for j in ORDER[1:]:
+    for j in ORDER:
+        out_copy(wrap(x + j)).start()
         for p in range(2):
             w_copy(p, wrap(x + j)).start()
+        if j == ORDER[0]:
+            for c in loads[2:]:
+                c.start()
 
     def remote(src, dst, send, recv, peer):
         return pltpu.make_async_remote_copy(
@@ -120,9 +122,12 @@
     n_tok = 2 * n_z - 1
     z_order = [1, n_z - 1] + list(range(2, n_z - 1))
 
+    def peers_of(count):
+        return (2, 1, 3) if count == SIDE else range(1, count)
+
     def exchange(e, peer_of, count, src, dst):
         return [remote(src(k), dst(k), ex_s.at[e * 8 + k], ex_r.at[e * 8 + k], peer_of(k))
-                for k in range(1, count)]
+                for k in peers_of(count)]
 
     started = []
 
@@ -144,17 +149,26 @@
             src, dst, i = qq.at[1, wrap(y + k), q], qr.at[1, k, q], SIDE + k * SIDE + j
         return remote(src, dst, q_s.at[i], q_r.at[i], ring1[p](k))
 
-    for i in range(2):
-        loads[i].wait()
+    cot_x = exchange(0, at_x, SIDE, lambda k: cot.at[:, quarter(wrap(x + k))], lambda k: cotq.at[x])
+
+    pl.semaphore_wait(barrier, len(peers))
+    loads[1].wait()
+    for i in z_order + [0]:
+        tok_copy(i).start()
+    for c in cot_x:
+        c.start()
+
+    loads[0].wait()
     for p in range(2):
         ain_t[p] = ainv[p].astype(F32).T.astype(BF16)
     step = min(128, depth)
 
     def prepare(m):
         q = wrap(x + offset(m))
+        out_copy(q).wait()
         for p in range(2):
             w_copy(p, q).wait()
-            left = aoutv[p, :, quarter(q)]
+            left = aoutv[q, p]
 
             def body(i, acc):
                 rows = pl.ds(pl.multiple_of(i * step, step), step)
@@ -176,8 +190,7 @@
     def q_send(m):
         j = offset(m)
 
-        @pl.when(m < SIDE - 1)
-        def _():
+        if not (isinstance(m, int) and m == SIDE - 1):
             q_first(0, j, 0).start()
 
         for k in (2, 1, 3):
@@ -185,32 +198,19 @@
 
     def early(m, carry):
         prepare(m)
+        q_send(m)
+
+        @pl.when(m == 0)
+        def _():
+            for i in z_order[:2]:
+                tok_copy(i).wait_recv()
+                tok_copy(n_z - 1 + i).start()
+
         return carry
 
     lax.fori_loop(0, 2, early, 0)
 
-    pl.semaphore_wait(barrier, len(peers))
-    loads[2].wait()
-    for i in z_order + [0]:
-        tok_copy(i).start()
-    cot_x = begin(exchange(0, at_x, SIDE, lambda k: cot.at[:, quarter(wrap(x + k))],
-                           lambda k: cotq.at[x]))
-
-    def early_send(m, carry):
-        q_send(m)
-        return carry
-
-    lax.fori_loop(0, 2, early_send, 0)
-
-    def later(m, carry):
-        prepare(m)
-        q_send(m)
-        return carry
-
-    lax.fori_loop(2, SIDE, later, 0)
-    ss_x = begin(exchange(1, at_x, SIDE, lambda k: ssb.at[wrap(x + k)], lambda k: ssr.at[k]))
-
-    for i in z_order:
+    for i in z_order[2:]:
         tok_copy(i).wait_recv()
         tok_copy(n_z - 1 + i).start()
     tok_copy(0).wait_recv()
@@ -254,49 +254,8 @@
         i = (p * 2 + d) * 3 + kind
         return remote(src, dst, ph2_s.at[i], ph2_r.at[i], peer)
 
+    ss_x = exchange(1, at_x, SIDE, lambda k: ssb.at[wrap(x + k)], lambda k: ssr.at[k])
     z_y = exchange(3, at_y, SIDE, lambda k: zb.at[wrap(y + k)], lambda k: zr.at[k])
-
-    def stage(i_p, carry):
-        j_p = offset(i_p)
-        q = wrap(x + j_p)
-        product(0, q)
-
-        @pl.when(i_p == 0)
-        def _():
-            for j in ORDER:
-                for d in range(2):
-                    main_copy(0, d, FAR, j).start()
-
-        @pl.when(i_p == 1)
-        def _():
-            for j in ORDER[:3]:
-                main_copy(0, 0, RAW, j).start()
-
-        @pl.when(i_p == 2)
-        def _():
-            for j in ORDER[:3]:
-                main_copy(0, 1, RAW, j).start()
-
-        product(1, q)
-        for d in range(2):
-            main_copy(1, d, FAR, j_p).start()
-
-        @pl.when(i_p < 3)
-        def _():
-            for d in range(2):
-                main_copy(1, d, RAW, j_p).start()
-
-        @pl.when(i_p == 0)
-        def _():
-            ain_all = ainv[...].reshape(2 * rank, depth)
-            for b in range(SIDE):
-                zb[b] = nt_dot(ain_all, lhs[b * tb:(b + 1) * tb, :]).astype(BF16)
-            for c in z_y:
-                c.start()
-
-        return carry
-
-    lax.fori_loop(0, SIDE, stage, 0)
 
     def add_into(dst, src):
         dst[...] = (dst[...].astype(F32) + src[...].astype(F32)).astype(BF16)
@@ -309,78 +268,128 @@
                 near = wrap(first[p] + (1 if d == 0 else -1))
                 add_into(pp.at[p, near, wrap(second[p] + j), rows, :], rfar.at[p, j, rows, :])
 
-    for j in ORDER[:3]:
-        accumulate(j)
+    def send_sums(j):
         for p in range(2):
             for d in range(2):
                 main_copy(p, d, ACC, j).start()
 
+    def finish(p, j):
+        for d in range(2):
+            main_copy(p, d, RAW, j).wait_recv()
+            main_copy(p, d, ACC, j).wait_recv()
+        mine = pp.at[p, first[p], wrap(second[p] + j)]
+        mine[...] = (mine[...].astype(F32) + rnear[p, 0, j].astype(F32)
+                     + rnear[p, 1, j].astype(F32)).astype(BF16)
+
+    def second_sum(p, d):
+        ph2_copy(p, d, FAR).wait_recv()
+        rows = top if d == 0 else bottom
+        near = wrap(second[p] + (1 if d == 0 else -1))
+        add_into(pp.at[p, first[p], near, rows, :], sfar.at[p, rows, :])
+        ph2_copy(p, d, ACC).start()
+
+    def stage(i_p, carry):
+        j_p = offset(i_p)
+        q = wrap(x + j_p)
+        product(0, q)
+
+        @pl.when(i_p == 0)
+        def _():
+            for j in ORDER:
+                for d in range(2):
+                    main_copy(0, d, FAR, j).start()
+
+        @pl.when(i_p == 1)
+        def _():
+            for j in ORDER[:3]:
+                main_copy(0, 0, RAW, j).start()
+
+        @pl.when(i_p == 2)
+        def _():
+            for j in ORDER[:3]:
+                main_copy(0, 1, RAW, j).start()
+
+        product(1, q)
+        for d in range(2):
+            main_copy(1, d, FAR, j_p).start()
+
+        @pl.when(i_p < 3)
+        def _():
+            for d in range(2):
+                main_copy(1, d, RAW, j_p).start()
+
+        @pl.when(i_p < 2)
+        def _():
+            prepare(i_p + 2)
+
+            @pl.when(i_p == 1)
+            def _():
+                for c in ss_x:
+                    c.start()
+
+        @pl.when(i_p == 2)
+        def _():
+            accumulate(2)
+            send_sums(2)
+
+        @pl.when(i_p == 3)
+        def _():
+            accumulate(1)
+            send_sums(1)
+
+        return carry
+
+    lax.fori_loop(0, SIDE, stage, 0)
+
+    accumulate(3)
+    send_sums(3)
+    ain_all = ainv[...].reshape(2 * rank, depth)
+    for b in range(SIDE):
+        zb[b] = nt_dot(ain_all, lhs[b * tb:(b + 1) * tb, :]).astype(BF16)
+    for c in z_y:
+        c.start()
+    accumulate(0)
+
+    for p in range(2):
+        finish(p, 2)
+        for d in range(2):
+            ph2_copy(p, d, FAR).start()
+    for p in range(2):
+        for d in range(2):
+            main_copy(p, d, RAW, 0).start()
+    for p in range(2):
+        finish(p, 1)
+        ph2_copy(p, 0, RAW).start()
     arrive(ss_x)
     ssx[...] = ssb[x] + ssr[1] + ssr[2] + ssr[3]
     ss_y = begin(exchange(2, at_y, SIDE, lambda k: ssx, lambda k: ssr2.at[k]))
+    for p in range(2):
+        second_sum(p, 0)
+    for p in range(2):
+        finish(p, 3)
+        ph2_copy(p, 1, RAW).start()
+    for p in range(2):
+        second_sum(p, 1)
+    for p in range(2):
+        for d in range(2):
+            main_copy(p, d, ACC, 0).start()
     arrive(z_y)
     zx[...] = (zb[y].astype(F32) + zr[1].astype(F32) + zr[2].astype(F32)
                + zr[3].astype(F32)).astype(BF16)
     z_x = begin(exchange(4, at_x, SIDE, lambda k: zx, lambda k: zr2.at[k]))
-    for k in (2, 1, 3):
-        q_first(0, k, 0).wait_recv()
-    for j in ORDER:
-        for k in (2, 1, 3):
-            q_first(1, k, j).wait_recv()
-    q_two = []
-    for p in range(2):
-        qx[p] = (qq[p, first[p]].astype(F32) + qr[p, 1].astype(F32) + qr[p, 2].astype(F32)
-                 + qr[p, 3].astype(F32)).astype(BF16)
-        q_two.append(begin(exchange(
-            17 + p, ring2[p], SIDE, lambda k, p=p: qx.at[p, wrap(second[p] + k)],
-            lambda k, p=p: qr2.at[p, k])))
-
-    def finish(j):
-        for p in range(2):
-            for d in range(2):
-                main_copy(p, d, RAW, j).wait_recv()
-                main_copy(p, d, ACC, j).wait_recv()
-            mine = pp.at[p, first[p], wrap(second[p] + j)]
-            mine[...] = (mine[...].astype(F32) + rnear[p, 0, j].astype(F32)
-                         + rnear[p, 1, j].astype(F32)).astype(BF16)
-
-    finish(2)
-    for p in range(2):
-        for d in range(2):
-            ph2_copy(p, d, FAR).start()
-    finish(1)
-    for p in range(2):
-        ph2_copy(p, 0, RAW).start()
-    finish(3)
-    for p in range(2):
-        ph2_copy(p, 1, RAW).start()
-    for p in range(2):
-        for d in range(2):
-            main_copy(p, d, RAW, 0).start()
-    accumulate(0)
-    for p in range(2):
-        for d in range(2):
-            ph2_copy(p, d, FAR).wait_recv()
-            rows = top if d == 0 else bottom
-            near = wrap(second[p] + (1 if d == 0 else -1))
-            add_into(pp.at[p, first[p], near, rows, :], sfar.at[p, rows, :])
-            ph2_copy(p, d, ACC).start()
-    for p in range(2):
-        for d in range(2):
-            main_copy(p, d, ACC, 0).start()
+    q_send(2)
+    q_send(3)
     arrive(ss_y)
     total = ssx[...] + ssr2[1] + ssr2[2] + ssr2[3]
     norm = jnp.sqrt(total + EPSILON)
-    loads[3].wait()
+    loads[2].wait()
     mag_q = magv[:, quarter(x)]
     coef = mag_q / norm
-    arrive(z_x)
-    zs[...] = (zx[...].astype(F32) + zr2[1].astype(F32) + zr2[2].astype(F32)
-               + zr2[3].astype(F32)).astype(BF16)
     arrive(cot_x)
-    loads[4].wait()
-
-    finish(0)
+    loads[3].wait()
+
+    for p in range(2):
+        finish(p, 0)
     for p in range(2):
         for d in range(2):
             ph2_copy(p, d, RAW).wait_recv()
@@ -418,23 +427,39 @@
     st_y = begin(exchange(6, at_y, SIDE, lambda k: st, lambda k: strr.at[k]))
 
     for p in range(2):
-        scaled = (aoutv[p, :, quarter(x)].astype(F32) * coef[p:p + 1]).astype(BF16)
+        scaled = (aoutv[x, p].astype(F32) * coef[p:p + 1]).astype(BF16)
         wv[p * rank:(p + 1) * rank, :] = nt_dot(scaled, dsc[p]).astype(BF16)
     w_x = begin(exchange(9, at_x, SIDE, lambda k: wv, lambda k: wr.at[k]))
+    arrive(z_x)
+    zs[...] = (zx[...].astype(F32) + zr2[1].astype(F32) + zr2[2].astype(F32)
+               + zr2[3].astype(F32)).astype(BF16)
     for p in range(2):
         res = jnp.dot(zs[p * rank:(p + 1) * rank, :], dsc[p], preferred_element_type=F32)
         for b in range(SIDE):
             g1[b, p] = res[b * rq:(b + 1) * rq, :].astype(BF16)
     g1_y = begin(exchange(8, at_y, SIDE, lambda k: g1.at[wrap(y + k)], lambda k: g1r.at[k]))
-    hid_x = begin(exchange(5, at_x, SIDE, lambda k: hidq.at[wrap(x + k)], lambda k: hidr.at[x]))
     hidr[x] = hidq[x]
 
+    for k in (2, 1, 3):
+        q_first(0, k, 0).wait_recv()
+    for j in ORDER:
+        for k in (2, 1, 3):
+            q_first(1, k, j).wait_recv()
+    for p in range(2):
+        qx[p] = (qq[p, first[p]].astype(F32) + qr[p, 1].astype(F32) + qr[p, 2].astype(F32)
+                 + qr[p, 3].astype(F32)).astype(BF16)
+    q_two = [
+        begin(exchange(17 + p, ring2[p], SIDE, lambda k, p=p: qx.at[p, wrap(second[p] + k)],
+                       lambda k, p=p: qr2.at[p, k]))
+        for p in range(2)
+    ]
     arrive(st_y)
     stat = st[...] + strr[1] + strr[2] + strr[3]
     tilt = mag_q * stat / (norm * norm * norm)
     bb[0:2] = tilt
     bb[2:4] = stat / norm
     b_x = begin(exchange(7, at_x, SIDE, lambda k: bb, lambda k: ball.at[x]))
+    hid_x = begin(exchange(5, at_x, SIDE, lambda k: hidq.at[wrap(x + k)], lambda k: hidr.at[x]))
     ball[x] = bb[...]
 
     arrive(w_x)
@@ -451,51 +476,69 @@
         low = (qx[p, second[p]].astype(F32) + qr2[p, 1].astype(F32) + qr2[p, 2].astype(F32)
                + qr2[p, 3].astype(F32))
         gall[p, second[p], first[p]] = (coef[p:p + 1] * both - tilt[p:p + 1] * low).astype(BF16)
-    ga_x = begin(exchange(11, at_x, SIDE, lambda k: gall.at[0, y, x], lambda k: gall.at[0, y, x]))
-    gb_y = begin(exchange(13, at_y, SIDE, lambda k: gall.at[1, x, y], lambda k: gall.at[1, x, y]))
+
+    def gat_one(p, k):
+        piece = gall.at[p, second[p], first[p]]
+        return remote(piece, piece, ex_s.at[(11 + p) * 8 + k], ex_r.at[(11 + p) * 8 + k],
+                      ring1[p](k))
+
+    def gat_two(p, i, k):
+        piece = gall.at[p, second[p], wrap(first[p] - i)]
+        n = (p * SIDE + i) * SIDE + k
+        return remote(piece, piece, gat_s.at[n], gat_r.at[n], ring2[p](k))
+
+    for k in (2, 1, 3):
+        for p in range(2):
+            gat_one(p, k).start()
+    for k in (2, 1, 3):
+        for p in range(2):
+            gat_two(p, 0, k).start()
 
     def tilted(p, q, b):
-        scaled = (aoutv[p, :, quarter(q)].astype(F32) * b).astype(BF16)
+        scaled = (aoutv[q, p].astype(F32) * b).astype(BF16)
         return nt_dot(scaled, wb[p, q])
 
     for p in range(2):
         tin[p] = -tilted(p, x, tilt[p:p + 1])
 
+    arrive(b_x)
+    out_rows = 2 * rank // n_row
+    for p in range(2):
+        t1 = tin[p]
+        for k in range(1, SIDE):
+            q = wrap(x + k)
+            t1 = t1 - tilted(p, q, ball[q, p:p + 1])
+        tin[p] = t1
     arrive(w_y)
     for p in range(2):
         t1 = tin[p]
         for b in range(SIDE):
             t1 = t1 + jnp.dot(wall[b, p * rank:(p + 1) * rank, :], lhs[b * tb:(b + 1) * tb, :],
                               preferred_element_type=F32)
-        tin[p] = t1
-
-    arrive(b_x)
-    out_rows = 2 * rank // n_row
-    for p in range(2):
-        t1 = tin[p]
-        for k in range(1, SIDE):
-            q = wrap(x + k)
-            t1 = t1 - tilted(p, q, ball[q, p:p + 1])
+
         for b in range(rank // out_rows):
             gib[p * (rank // out_rows) + b] = t1[b * out_rows:(b + 1) * out_rows].astype(BF16)
     gi_rs = begin(exchange(15, at_row, n_row, lambda k: gib.at[(row + k) % n_row],
                            lambda k: gir.at[k]))
 
-    arrive(ga_x)
-    ga_y = begin(exchange(12, at_y, SIDE, lambda k: gall.at[0, y], lambda k: gall.at[0, y]))
-    arrive(gb_y)
-    gb_x = begin(exchange(14, at_x, SIDE, lambda k: gall.at[1, x], lambda k: gall.at[1, x]))
+    for i in (1, 3, 2):
+        for p in range(2):
+            gat_one(p, i).wait_recv()
+            for k in (2, 1, 3):
+                gat_two(p, i, k).start()
     for q in range(SIDE):
-        gmq[q] = ball[q, 2:4, :]
-    arrive(hid_x)
+        gmq[:, q * fq:(q + 1) * fq] = ball[q, 2:4, :]
     outs = [
         pltpu.make_async_copy(gmq, gm_out, out_sem.at[0]),
-        pltpu.make_async_copy(hidr, hid_out, out_sem.at[1]),
-        pltpu.make_async_copy(gall, go_out, out_sem.at[2]),
-        pltpu.make_async_copy(giall, gi_out, out_sem.at[3]),
+        pltpu.make_async_copy(giall, gi_out, out_sem.at[1]),
+        pltpu.make_async_copy(gall.at[0], go_out.at[0], out_sem.at[2]),
+        pltpu.make_async_copy(gall.at[1], go_out.at[1], out_sem.at[3]),
+    ]
+    hid_outs = [
+        pltpu.make_async_copy(hidr.at[q], hid_out.at[:, q * fq:(q + 1) * fq], hid_sem.at[q])
+        for q in range(SIDE)
     ]
     outs[0].start()
-    outs[1].start()
 
     arrive(gi_rs)
     acc = gib[row].astype(F32)
@@ -504,17 +547,27 @@
     gio[...] = acc.astype(BF16)
     gi_ag = begin(exchange(16, at_row, n_row, lambda k: gio, lambda k: giall.at[row]))
     giall[row] = gio[...]
-
-    arrive(ga_y)
-    arrive(gb_x)
-    outs[2].start()
+    arrive(hid_x)
+    for c in hid_outs:
+        c.start()
+
+    for p in range(2):
+        for i in range(SIDE):
+            for k in (1, 2, 3):
+                gat_two(p, i, k).wait_recv()
+        outs[2 + p].start()
     arrive(gi_ag)
-    outs[3].start()
+    outs[1].start()
 
     for i in range(n_tok):
         tok_copy(i).wait_send()
-    for c in z_y:
+    for c in cot_x + ss_x + z_y:
         c.wait_send()
+    for p in range(2):
+        for k in (1, 2, 3):
+            gat_one(p, k).wait_send()
+            for i in range(SIDE):
+                gat_two(p, i, k).wait_send()
     for k in (1, 2, 3):
         q_first(0, k, 0).wait_send()
         for j in range(SIDE):
@@ -527,25 +580,48 @@
                 ph2_copy(p, d, kind).wait_send()
     for c in started:
         c.wait_send()
+    for c in outs + hid_outs:
+        c.wait()
+
+
+def finish_kernel(hid_in, gi_in, go_in, gm_in, hid, gi, go, gm,
+                  hid_v, gi_v, go_v, gm_v, gi_f, go_f, in_sem, out_sem):
+    n_row, out_rows = gi_in.shape[:2]
+    rq, fq = go_in.shape[3:]
+    per = n_row // 2
+    loads = [
+        pltpu.make_async_copy(go_in.at[0], go_v.at[0], in_sem.at[0]),
+        pltpu.make_async_copy(go_in.at[1], go_v.at[1], in_sem.at[1]),
+        pltpu.make_async_copy(gi_in, gi_v, in_sem.at[2]),
+        pltpu.make_async_copy(hid_in, hid_v, in_sem.at[3]),
+        pltpu.make_async_copy(gm_in, gm_v, in_sem.at[4]),
+    ]
+    outs = [
+        pltpu.make_async_copy(go_f.at[0], go.at[0], out_sem.at[0]),
+        pltpu.make_async_copy(go_f.at[1], go.at[1], out_sem.at[1]),
+        pltpu.make_async_copy(gi_f, gi, out_sem.at[2]),
+        pltpu.make_async_copy(hid_v, hid, out_sem.at[3]),
+        pltpu.make_async_copy(gm_v, gm, out_sem.at[4]),
+    ]
+    for c in loads:
+        c.start()
+    for p in range(2):
+        loads[p].wait()
+        for q in range(SIDE):
+            for b in range(SIDE):
+                piece = go_v[0, b, q] if p == 0 else go_v[1, q, b]
+                go_f[p, b * rq:(b + 1) * rq, q * fq:(q + 1) * fq] = piece.astype(F32)
+        outs[p].start()
+    for i in (3, 4):
+        loads[i].wait()
+        outs[i].start()
+    loads[2].wait()
+    for p in range(2):
+        for b in range(per):
+            gi_f[p, b * out_rows:(b + 1) * out_rows, :] = gi_v[p * per + b].astype(F32)
+    outs[2].start()
     for c in outs:
         c.wait()
-
-
-def finish_kernel(hidr, giall, gall, gmq, hid, gi, go, gm):
-    fq = hidr.shape[2]
-    rq = gall.shape[3]
-    n_row, out_rows = giall.shape[:2]
-    per = n_row // 2
-    for q in range(SIDE):
-        lanes = slice(q * fq, (q + 1) * fq)
-        hid[:, lanes] = hidr[q]
-        gm[:, lanes] = gmq[q]
-        for b in range(SIDE):
-            go[0, b * rq:(b + 1) * rq, lanes] = gall[0, b, q].astype(F32)
-            go[1, b * rq:(b + 1) * rq, lanes] = gall[1, q, b].astype(F32)
-    for p in range(2):
-        for b in range(per):
-            gi[p, b * out_rows:(b + 1) * out_rows, :] = giall[p * per + b].astype(F32)
 
 
 def solution(mesh):
@@ -567,7 +643,7 @@
             vm((2, SIDE, depth, fq), BF16),
             vm((2, SIDE, SIDE, tb, fq), BF16),
             vm((2, rank, depth), BF16),
-            vm((2, rank, width), BF16),
+            vm((SIDE, 2, rank, fq), BF16),
             vm((2, width), F32),
             vm((2, depth, rank), BF16),
             vm((2, SIDE, tb, fq), BF16),
@@ -591,7 +667,7 @@
             vm((SIDE, 2, fq), F32),
             vm((4, fq), F32),
             vm((SIDE, 4, fq), F32),
-            vm((SIDE, 2, fq), F32),
+            vm((2, width), F32),
             vm((SIDE, 2, rq, fq), BF16),
             vm((SIDE, 2, rq, fq), BF16),
             vm((pr, tb), BF16),
@@ -609,8 +685,12 @@
             vm((n_row, pr // n_row, depth), BF16),
             vm((2, rank, depth), F32),
             dma((2 * SIDE,)),
-            dma((5,)),
+            dma((SIDE,)),
             dma((4,)),
+            dma((4,)),
+            dma((SIDE,)),
+            dma((2 * SIDE * SIDE,)),
+            dma((2 * SIDE * SIDE,)),
             dma((n_row,)),
             dma((n_row,)),
             dma((12 * SIDE,)),
@@ -626,10 +706,10 @@
         parts = pl.pallas_call(
             functools.partial(kernel, n_row),
             out_shape=(
-                jax.ShapeDtypeStruct((SIDE, own_rows, fq), BF16),
+                jax.ShapeDtypeStruct(hidden_cot.shape, BF16),
                 jax.ShapeDtypeStruct((n_row, pr // n_row, depth), BF16),
                 jax.ShapeDtypeStruct((2, SIDE, SIDE, rq, fq), BF16),
-                jax.ShapeDtypeStruct((SIDE, 2, fq), F32),
+                jax.ShapeDtypeStruct(magnitude.shape, F32),
             ),
             in_specs=[anywhere] * 6,
             out_specs=(anywhere,) * 4,
@@ -646,6 +726,19 @@
                 jax.ShapeDtypeStruct(adapter_out.shape, F32),
                 jax.ShapeDtypeStruct(magnitude.shape, F32),
             ),
+            in_specs=[anywhere] * 4,
+            out_specs=(anywhere,) * 4,
+            scratch_shapes=[
+                vm(hidden_cot.shape, BF16),
+                vm((n_row, pr // n_row, depth), BF16),
+                vm((2, SIDE, SIDE, rq, fq), BF16),
+                vm(magnitude.shape, F32),
+                vm(adapter_in.shape, F32),
+                vm(adapter_out.shape, F32),
+                dma((5,)),
+                dma((5,)),
+            ],
+            compiler_params=pltpu.CompilerParams(vmem_limit_bytes=67_043_328),
         )(*parts)
 
     in_specs = (

time: 91.4 us -> 87.3 us (0.955)
  Pallas kernels: 90.6 us -> 86.5 us
    pallas_call x1, Pallas kernels: 87.8 us -> 83.9 us  [on_device(): pl.pallas_call(functools.partial(kernel, n_row), out_shape=(jax.ShapeDtyp...]
where the time goes in v4:
time: 87.3 us; the launch traced here: 87.1 us
  Pallas kernels  86.5 us (99%)
    pallas_call x1, Pallas kernels, on_device(): pl.pallas_call(functools.partial(kernel, n_row), out_shape=(jax.ShapeDtyp...  83.9 us
    pallas_call x1, Pallas kernels, on_device(): pl.pallas_call(finish_kernel, out_shape=(jax.ShapeDtypeStruct(hidden_cot....  2.56 us

profile of v4, /device:TPU:1, one launch (start us, length us, event | category | flops | bytes accessed | tf_op | source)
XLA Modules:
  0.0 87.1 jit_solution(9893161950343284232)
XLA Ops:
  0.6 83.9 %shard_map.93 = (bf16[32,3584]{1,0:T(8,128)(2,1)}, bf16[8,16,512]{2,1,0:T(8,128)(2,1)}, bf16[2,4,4,16,896]{4,3,2,1,0:T(8,128)(2,1)}, f32[2,3584]{1,0:T(2,128)}) custom-call(bf16[64,512]{1,0:T(8,128)(2,1)} %tok.1, bf16[2,512,3584]{2,1,0:T(8,128)(2,1)} %w_hbm.1, bf16[2,64,512]{2,1,0:T(8,128)(2,1)} %ain.1, bf16[2,64,3584]{2,1,0:T(8,128)(2,1)} %aout.1, ...), custom_call_target="tpu_custom_call" | custom-call | tf_op jit(solution)/shard_map/pallas_call | solution.py:706
  84.6 2.6 %shard_map.94 = (bf16[32,3584]{1,0:T(8,128)(2,1)}, f32[2,64,512]{2,1,0:T(8,128)}, f32[2,64,3584]{2,1,0:T(8,128)}, f32[2,3584]{1,0:T(2,128)}) custom-call(bf16[32,3584]{1,0:T(8,128)(2,1)} %get-tuple-element.8.hid_in, bf16[8,16,512]{2,1,0:T(8,128)(2,1)} %get-tuple-element.9.gi_in, bf16[2,4,4,16,896]{4,3,2,1,0:T(8,128)(2,1)} %get-tuple-element.10.go_in, ...), custom_call_target="tpu_custom_call" | custom-call | tf_op jit(solution)/shard_map/pallas_call | solution.py:721

commit v5 on v4

--- a/solution.py
+++ b/solution.py
@@ -21,11 +21,11 @@
     return lax.dot_general(a, b, (((1,), (1,)), ((), ())), preferred_element_type=F32)
 
 
-def kernel(n_row, tok, w_hbm, ain, aout, mag, cot, hid_out, gi_out, go_out, gm_out,
+def kernel(n_row, tok, w_hbm, ain, aout, mag, cot, hid_out, giall, gall, gm_out,
            lhs, wb, pp, ainv, aoutv, magv, ain_t, rfar, rnear, sfar, snear, cotq, ssb, ssx, ssr, ssr2,
-           zb, zx, zs, zr, zr2, hidq, hidr, dsc, st, strr, bb, ball, gmq, g1, g1r,
-           wv, wx, wr, wall, qq, qr, qx, qr2, gall, gib, gir, gio, giall, tin,
-           w_sem, a_sem, in_sem, out_sem, hid_sem, gat_s, gat_r, tok_s, tok_r, main_s, main_r, ph2_s, ph2_r, q_s, q_r, ex_s, ex_r):
+           zb, zx, zs, zr, zr2, hidq, hidr, dsc, st, strr, bb, ball, g1, g1r,
+           wv, wx, wr, wall, qq, qr, qx, qr2, gib, gir, gio, tin,
+           w_sem, a_sem, in_sem, gat_s, gat_r, tok_s, tok_r, main_s, main_r, ph2_s, ph2_r, q_s, q_r, ex_s, ex_r):
     row, col = lax.axis_index("row"), lax.axis_index("col")
     y, x = col // SIDE, col % SIDE
     n_z = n_row // 2
@@ -120,7 +120,7 @@
         return remote(tok_rows(owner), tok_rows(owner), tok_s.at[i], tok_r.at[i], peer)
 
     n_tok = 2 * n_z - 1
-    z_order = [1, n_z - 1] + list(range(2, n_z - 1))
+    z_order = list(range(2, n_z - 1)) + [1, n_z - 1]
 
     def peers_of(count):
         return (2, 1, 3) if count == SIDE else range(1, count)
@@ -200,17 +200,11 @@
         prepare(m)
         q_send(m)
 
-        @pl.when(m == 0)
-        def _():
-            for i in z_order[:2]:
-                tok_copy(i).wait_recv()
-                tok_copy(n_z - 1 + i).start()
-
         return carry
 
     lax.fori_loop(0, 2, early, 0)
 
-    for i in z_order[2:]:
+    for i in z_order:
         tok_copy(i).wait_recv()
         tok_copy(n_z - 1 + i).start()
     tok_copy(0).wait_recv()
@@ -291,6 +285,15 @@
     def stage(i_p, carry):
         j_p = offset(i_p)
         q = wrap(x + j_p)
+        product(1, q)
+        for d in range(2):
+            main_copy(1, d, FAR, j_p).start()
+
+        @pl.when(i_p < 3)
+        def _():
+            for d in range(2):
+                main_copy(1, d, RAW, j_p).start()
+
         product(0, q)
 
         @pl.when(i_p == 0)
@@ -308,15 +311,6 @@
         def _():
             for j in ORDER[:3]:
                 main_copy(0, 1, RAW, j).start()
-
-        product(1, q)
-        for d in range(2):
-            main_copy(1, d, FAR, j_p).start()
-
-        @pl.when(i_p < 3)
-        def _():
-            for d in range(2):
-                main_copy(1, d, RAW, j_p).start()
 
         @pl.when(i_p < 2)
         def _():
@@ -468,6 +462,13 @@
     w_y = begin(exchange(10, at_y, SIDE, lambda k: wx, lambda k: wall.at[y]))
     wall[y] = wx[...]
 
+    def tilted(p, q, b):
+        scaled = (aoutv[q, p].astype(F32) * b).astype(BF16)
+        return nt_dot(scaled, wb[p, q])
+
+    for p in range(2):
+        tin[p] = -tilted(p, x, tilt[p:p + 1])
+
     arrive(g1_y)
     for p in range(2):
         arrive(q_two[p])
@@ -494,13 +495,6 @@
         for p in range(2):
             gat_two(p, 0, k).start()
 
-    def tilted(p, q, b):
-        scaled = (aoutv[q, p].astype(F32) * b).astype(BF16)
-        return nt_dot(scaled, wb[p, q])
-
-    for p in range(2):
-        tin[p] = -tilted(p, x, tilt[p:p + 1])
-
     arrive(b_x)
     out_rows = 2 * rank // n_row
     for p in range(2):
@@ -527,19 +521,7 @@
             for k in (2, 1, 3):
                 gat_two(p, i, k).start()
     for q in range(SIDE):
-        gmq[:, q * fq:(q + 1) * fq] = ball[q, 2:4, :]
-    outs = [
-        pltpu.make_async_copy(gmq, gm_out, out_sem.at[0]),
-        pltpu.make_async_copy(giall, gi_out, out_sem.at[1]),
-        pltpu.make_async_copy(gall.at[0], go_out.at[0], out_sem.at[2]),
-        pltpu.make_async_copy(gall.at[1], go_out.at[1], out_sem.at[3]),
-    ]
-    hid_outs = [
-        pltpu.make_async_copy(hidr.at[q], hid_out.at[:, q * fq:(q + 1) * fq], hid_sem.at[q])
-        for q in range(SIDE)
-    ]
-    outs[0].start()
-
+        gm_out[:, q * fq:(q + 1) * fq] = ball[q, 2:4, :]
     arrive(gi_rs)
     acc = gib[row].astype(F32)
     for k in range(1, n_row):
@@ -548,16 +530,14 @@
     gi_ag = begin(exchange(16, at_row, n_row, lambda k: gio, lambda k: giall.at[row]))
     giall[row] = gio[...]
     arrive(hid_x)
-    for c in hid_outs:
-        c.start()
+    for q in range(SIDE):
+        hid_out[:, q * fq:(q + 1) * fq] = hidr[q]
 
     for p in range(2):
         for i in range(SIDE):
             for k in (1, 2, 3):
                 gat_two(p, i, k).wait_recv()
-        outs[2 + p].start()
     arrive(gi_ag)
-    outs[1].start()
 
     for i in range(n_tok):
         tok_copy(i).wait_send()
@@ -580,45 +560,30 @@
                 ph2_copy(p, d, kind).wait_send()
     for c in started:
         c.wait_send()
-    for c in outs + hid_outs:
-        c.wait()
-
-
-def finish_kernel(hid_in, gi_in, go_in, gm_in, hid, gi, go, gm,
-                  hid_v, gi_v, go_v, gm_v, gi_f, go_f, in_sem, out_sem):
+
+
+def finish_kernel(hid_in, gi_in, go_in, gm_in, hid, gi, go, gm, gi_f, go_f, out_sem):
     n_row, out_rows = gi_in.shape[:2]
     rq, fq = go_in.shape[3:]
     per = n_row // 2
-    loads = [
-        pltpu.make_async_copy(go_in.at[0], go_v.at[0], in_sem.at[0]),
-        pltpu.make_async_copy(go_in.at[1], go_v.at[1], in_sem.at[1]),
-        pltpu.make_async_copy(gi_in, gi_v, in_sem.at[2]),
-        pltpu.make_async_copy(hid_in, hid_v, in_sem.at[3]),
-        pltpu.make_async_copy(gm_in, gm_v, in_sem.at[4]),
-    ]
     outs = [
         pltpu.make_async_copy(go_f.at[0], go.at[0], out_sem.at[0]),
         pltpu.make_async_copy(go_f.at[1], go.at[1], out_sem.at[1]),
         pltpu.make_async_copy(gi_f, gi, out_sem.at[2]),
-        pltpu.make_async_copy(hid_v, hid, out_sem.at[3]),
-        pltpu.make_async_copy(gm_v, gm, out_sem.at[4]),
+        pltpu.make_async_copy(hid_in, hid, out_sem.at[3]),
+        pltpu.make_async_copy(gm_in, gm, out_sem.at[4]),
     ]
-    for c in loads:
-        c.start()
-    for p in range(2):
-        loads[p].wait()
+    for p in range(2):
         for q in range(SIDE):
             for b in range(SIDE):
-                piece = go_v[0, b, q] if p == 0 else go_v[1, q, b]
+                piece = go_in[0, b, q] if p == 0 else go_in[1, q, b]
                 go_f[p, b * rq:(b + 1) * rq, q * fq:(q + 1) * fq] = piece.astype(F32)
         outs[p].start()
-    for i in (3, 4):
-        loads[i].wait()
-        outs[i].start()
-    loads[2].wait()
+    outs[3].start()
+    outs[4].start()
     for p in range(2):
         for b in range(per):
-            gi_f[p, b * out_rows:(b + 1) * out_rows, :] = gi_v[p * per + b].astype(F32)
+            gi_f[p, b * out_rows:(b + 1) * out_rows, :] = gi_in[p * per + b].astype(F32)
     outs[2].start()
     for c in outs:
         c.wait()
@@ -667,7 +632,6 @@
             vm((SIDE, 2, fq), F32),
             vm((4, fq), F32),
             vm((SIDE, 4, fq), F32),
-            vm((2, width), F32),
             vm((SIDE, 2, rq, fq), BF16),
             vm((SIDE, 2, rq, fq), BF16),
             vm((pr, tb), BF16),
@@ -678,17 +642,13 @@
             vm((2, SIDE, SIDE, rq, fq), BF16),
             vm((2, SIDE, rq, fq), BF16),
             vm((2, SIDE, rq, fq), BF16),
-            vm((2, SIDE, SIDE, rq, fq), BF16),
             vm((n_row, pr // n_row, depth), BF16),
             vm((n_row, pr // n_row, depth), BF16),
             vm((pr // n_row, depth), BF16),
-            vm((n_row, pr // n_row, depth), BF16),
             vm((2, rank, depth), F32),
             dma((2 * SIDE,)),
             dma((SIDE,)),
             dma((4,)),
-            dma((4,)),
-            dma((SIDE,)),
             dma((2 * SIDE * SIDE,)),
             dma((2 * SIDE * SIDE,)),
             dma((n_row,)),
@@ -703,6 +663,7 @@
             dma((EXCHANGES * 8,)),
         ]
         anywhere = pl.BlockSpec(memory_space=pl.ANY)
+        arrays = (tokens, weights, adapter_in, adapter_out, magnitude, hidden_cot)
         parts = pl.pallas_call(
             functools.partial(kernel, n_row),
             out_shape=(
@@ -711,13 +672,13 @@
                 jax.ShapeDtypeStruct((2, SIDE, SIDE, rq, fq), BF16),
                 jax.ShapeDtypeStruct(magnitude.shape, F32),
             ),
-            in_specs=[anywhere] * 6,
-            out_specs=(anywhere,) * 4,
+            in_specs=[pl.BlockSpec(memory_space=pltpu.HBM)] * 6,
+            out_specs=(pl.BlockSpec(memory_space=pltpu.VMEM),) * 4,
             scratch_shapes=scratch,
             compiler_params=pltpu.CompilerParams(
-                collective_id=0, has_side_effects=True, vmem_limit_bytes=67_043_328
+                collective_id=0, has_side_effects=True, vmem_limit_bytes=44 * 2**20
             ),
-        )(tokens, weights, adapter_in, adapter_out, magnitude, hidden_cot)
+        )(*[pltpu.with_memory_space_constraint(a, pltpu.HBM) for a in arrays])
         return pl.pallas_call(
             finish_kernel,
             out_shape=(
@@ -726,19 +687,14 @@
                 jax.ShapeDtypeStruct(adapter_out.shape, F32),
                 jax.ShapeDtypeStruct(magnitude.shape, F32),
             ),
-            in_specs=[anywhere] * 4,
+            in_specs=[pl.BlockSpec(memory_space=pltpu.VMEM)] * 4,
             out_specs=(anywhere,) * 4,
             scratch_shapes=[
-                vm(hidden_cot.shape, BF16),
-                vm((n_row, pr // n_row, depth), BF16),
-                vm((2, SIDE, SIDE, rq, fq), BF16),
-                vm(magnitude.shape, F32),
                 vm(adapter_in.shape, F32),
                 vm(adapter_out.shape, F32),
                 dma((5,)),
-                dma((5,)),
             ],
-            compiler_params=pltpu.CompilerParams(vmem_limit_bytes=67_043_328),
+            compiler_params=pltpu.CompilerParams(vmem_limit_bytes=8 * 2**20),
         )(*parts)
 
     in_specs = (

time: 87.3 us -> 84.2 us (0.964)
  Pallas kernels: 86.5 us -> 83.5 us
    pallas_call x1, Pallas kernels: 83.9 us -> 82 us  [on_device(): pl.pallas_call(functools.partial(kernel, n_row), out_shape=(jax.ShapeDtyp...]
    pallas_call x1, Pallas kernels: 2.56 us -> 1.5 us  [on_device(): pl.pallas_call(finish_kernel, out_shape=(jax.ShapeDtypeStruct(hidden_cot....]
where the time goes in v5:
time: 84.2 us; the launch traced here: 84.1 us
  Pallas kernels  83.5 us (99%)
    pallas_call x1, Pallas kernels, on_device(): pl.pallas_call(functools.partial(kernel, n_row), out_shape=(jax.ShapeDtyp...  82 us

profile of v5, /device:TPU:1, one launch (start us, length us, event | category | flops | bytes accessed | tf_op | source)
XLA Modules:
  0.0 84.1 jit_solution(3866947561821047737)
XLA Ops:
  0.6 82.0 %shard_map.93 = (bf16[32,3584]{1,0:T(8,128)(2,1)S(1)}, bf16[8,16,512]{2,1,0:T(8,128)(2,1)S(1)}, bf16[2,4,4,16,896]{4,3,2,1,0:T(8,128)(2,1)S(1)}, f32[2,3584]{1,0:T(2,128)S(1)}) custom-call(bf16[64,512]{1,0:T(8,128)(2,1)} %tok.1, bf16[2,512,3584]{2,1,0:T(8,128)(2,1)} %w_hbm.1, bf16[2,64,512]{2,1,0:T(8,128)(2,1)} %ain.1, bf16[2,64,3584]{2,1,0:T(8,128)(2,1)} %aout.1, ...), custom_call_target="tpu_custom_call" | custom-call | tf_op jit(solution)/shard_map/pallas_call | solution.py:667
  82.6 1.5 %shard_map.94 = (bf16[32,3584]{1,0:T(8,128)(2,1)}, f32[2,64,512]{2,1,0:T(8,128)}, f32[2,64,3584]{2,1,0:T(8,128)}, f32[2,3584]{1,0:T(2,128)}) custom-call(bf16[32,3584]{1,0:T(8,128)(2,1)S(1)} %get-tuple-element.8.hid_in, bf16[8,16,512]{2,1,0:T(8,128)(2,1)S(1)} %get-tuple-element.9.gi_in, bf16[2,4,4,16,896]{4,3,2,1,0:T(8,128)(2,1)S(1)} %get-tuple-element.10.go_in, ...), custom_call_target="tpu_custom_call" | custom-call | tf_op jit(solution)/shard_map/pallas_call | solution.py:682
